TPU v7x, 32 devices: a whole 2x2x4 slice. The times are simulated.
32 devices in a mesh: seq: 16 (over z, y, core), head: 2 (over x).
Axes of the slice: x: 2, y: 2, z: 4, core: 2. Of those that a mesh axis runs over, the one named last changes fastest.
Arguments:
- tokens: bfloat16 [16384, 768], P(('seq', 'head')), may hold values from -6 to 6
- w_query: bfloat16 [768, 768], replicated, may hold values from -0.3125 to 0.3125
- w_key: bfloat16 [768, 768], replicated, may hold values from -0.21875 to 0.21875
- w_value: bfloat16 [768, 768], replicated, may hold values from -0.21875 to 0.21875
- w_out: bfloat16 [768, 768], replicated, may hold values from -3.5 to 3.5
- gain_attn: float32 [768], replicated, may hold values from 0.5 to 1.5
- shift_attn: float32 [768], replicated, may hold values from -3 to 3
- w_up: bfloat16 [768, 3072], replicated, may hold values from -0.21875 to 0.21875
- w_down: bfloat16 [3072, 768], replicated, may hold values from -0.109375 to 0.109375
- gain_mlp: float32 [768], replicated, may hold values from 0.5 to 1.5
- shift_mlp: float32 [768], replicated, may hold values from -3 to 3
- cotangent: bfloat16 [16384, 768], P(('seq', 'head')), may hold values from -6 to 6
- lengths: int32 [8], replicated, may hold values from 1 to 64, 256 in all
- seq_order: int32 [8], replicated, may hold values from 0 to 7, each once
- rand_blocks: int32 [256, 3], P('seq'), may hold values from 0 to 65535
Outputs:
- output: bfloat16 [16384, 768], P(('seq', 'head'))
- grad_tokens: float32 [16384, 768], P(('seq', 'head'))
- grad_w_query: float32 [768, 768], P('seq')
- grad_w_key: float32 [768, 768], P('seq')
- grad_w_value: float32 [768, 768], P('seq')
- grad_w_out: float32 [768, 768], P('seq')
- grad_gain_attn: float32 [768], P('seq')
- grad_shift_attn: float32 [768], P('seq')
- grad_w_up: float32 [768, 3072], P('seq')
- grad_w_down: float32 [3072, 768], P('seq')
- grad_gain_mlp: float32 [768], P('seq')
- grad_shift_mlp: float32 [768], P('seq')
Inputs may be any that keep to these rules, and one draw needn't show every extreme that they name: lengths of the 8 sequences in blocks of 64 tokens; they sum to 256 and the longest is exactly 64. `seq_order`: each of 0 to 7 once.
All inputs are finite; a program needn't handle non-finite values.
Results may differ from a plain program's by a relative error of at most 0.017.
Values may be sent and summed in bfloat16 or wider, within the bound.
A program may use at most 320 MiB of HBM per device.

v0:
```python
import functools

import jax
import jax.numpy as jnp
from jax import lax
from jax.experimental import pallas as pl
from jax.experimental.pallas import tpu as pltpu
from jax.sharding import PartitionSpec as P

DH = 64
BLK = 64
MAXB = 64
SLOTS = 8
HG = 3
WQ = HG * DH
WIN = 256
AXES = ("seq", "head")
NEG = -1e30

eps_norm = 1e-06


def xor_swap(value, bits):
    count = lax.axis_size("seq") * lax.axis_size("head")
    return lax.ppermute(value, AXES, [(d, d ^ bits) for d in range(count)])


def lane_groups(rows, offset):
    lane = lax.broadcasted_iota(jnp.int32, (rows, WIN), 1) - offset
    return [jnp.logical_and(lane >= h * DH, lane < (h + 1) * DH) for h in range(HG)]


def spread_heads(block, offset):
    zero = jnp.zeros_like(block)
    return jnp.concatenate([jnp.where(m, block, zero) for m in lane_groups(BLK, offset)], axis=0)


def fold_heads(stacked, offset):
    masks = lane_groups(BLK, offset)
    total = jnp.where(masks[0], stacked[:BLK], 0.0)
    for h in range(1, HG):
        total = total + jnp.where(masks[h], stacked[h * BLK : (h + 1) * BLK], 0.0)
    return total


def nt(a, b):
    return lax.dot_general(a, b, (((1,), (1,)), ((), ())), preferred_element_type=jnp.float32)


def tn(a, b):
    return lax.dot_general(a, b, (((0,), (0,)), ((), ())), preferred_element_type=jnp.float32)


def backward_kernel(idx_ref, live_ref, q_ref, do_ref, lse_ref, *refs):
    kv_ref, dq_ref, dkv_ref, kv, acc, sems = refs

    def clear(n, carry):
        acc[pl.ds(pl.multiple_of(n * 256, 256), 256), :] = jnp.zeros((256, 2 * WQ), jnp.float32)
        return carry

    copy = pltpu.make_async_copy(kv_ref, kv, sems.at[0])
    copy.start()
    lax.fori_loop(0, acc.shape[0] // 256, clear, 0)
    copy.wait()

    def step(i, carry):
        q_rows = pl.multiple_of(i * BLK, BLK)
        qexp = spread_heads(q_ref[pl.ds(q_rows, BLK), :], 0)
        doexp = spread_heads(do_ref[pl.ds(q_rows, BLK), :], 64)
        rows = [
            pl.multiple_of(idx_ref[i * SLOTS + s] * BLK, BLK) for s in range(SLOTS)
        ]
        keys = jnp.concatenate([kv[pl.ds(r, BLK), 0:WIN] for r in rows], axis=0)
        values = jnp.concatenate([kv[pl.ds(r, BLK), 128 : 128 + WIN] for r in rows], axis=0)
        raw = nt(keys, qexp)
        level = lse_ref[pl.ds(i, 1), :]
        probs = jnp.concatenate(
            [
                jnp.exp(
                    raw[s * BLK : (s + 1) * BLK]
                    - (level + jnp.where(live_ref[i * SLOTS + s] > 0, 0.0, -NEG))
                )
                for s in range(SLOTS)
            ],
            axis=0,
        )
        grad_probs = nt(values, doexp)
        inner = jnp.sum(probs * grad_probs, axis=0, keepdims=True)
        grad_scores = (probs * (grad_probs - inner)).astype(jnp.bfloat16)
        dk = jnp.dot(grad_scores, qexp, preferred_element_type=jnp.float32)
        dv = jnp.dot(probs.astype(jnp.bfloat16), doexp, preferred_element_type=jnp.float32)
        dq = tn(grad_scores, keys)
        dq_ref[pl.ds(q_rows, BLK), :] = (fold_heads(dq, 0) * DH ** (-0.5)).astype(jnp.bfloat16)
        for s in range(SLOTS):
            k_s, v_s = dk[s * BLK : (s + 1) * BLK], dv[s * BLK : (s + 1) * BLK]
            at = pl.ds(rows[s], BLK)
            acc[at, 0:128] += k_s[:, :128]
            acc[at, 128:256] += k_s[:, 128:] + v_s[:, :128]
            acc[at, 256:384] += v_s[:, 128:]
        return carry

    lax.fori_loop(0, q_ref.shape[0] // BLK, step, 0, unroll=4)

    def emit(n, carry):
        at = pl.ds(pl.multiple_of(n * 256, 256), 256)
        dkv_ref[at, :] = acc[at, :].astype(jnp.bfloat16)
        return carry

    lax.fori_loop(0, acc.shape[0] // 256, emit, 0)


VMEM = pl.BlockSpec(memory_space=pltpu.VMEM)
SMEM = pl.BlockSpec(memory_space=pltpu.SMEM)
ANY = pl.BlockSpec(memory_space=pl.ANY)


def device_at(plane, y_at, core, x_at):
    return (plane * 4 + y_at * 2 + core, x_at)


def place():
    seq_at, x_at = lax.axis_index("seq"), lax.axis_index("head")
    return seq_at // 4, (seq_at // 2) % 2, seq_at % 2, x_at


def remote(src, dst, sems, recvs, at, device):
    return pltpu.make_async_remote_copy(
        src_ref=src,
        dst_ref=dst,
        send_sem=sems.at[at],
        recv_sem=recvs.at[at],
        device_id=device,
        device_id_type=pl.DeviceIdType.MESH,
    )


def greet(partners):
    barrier = pltpu.get_barrier_semaphore()
    for device in partners:
        pl.semaphore_signal(
            barrier, inc=1, device_id=device, device_id_type=pl.DeviceIdType.MESH
        )
    pl.semaphore_wait(barrier, len(partners))


CHUNK_ORDER = (0, 1, 2, 4, 3, 5, 6, 7)
JORDER = (3, 1, 2, 0)


def slot_tables(plane, y_at, core, x_at, at, lengths, order, rand_own, rand_got, idx_ref, live_ref):
    per = at["piece_blocks"]

    def one(i, carry):
        far, near = i // per, i % per
        y_of, x_of = y_at ^ (far >> 1), x_at ^ (far & 1)
        block = plane * MAXB + y_of * (4 * per) + core * (2 * per) + x_of * per + near
        begin, first, span = jnp.int32(0), jnp.int32(0), jnp.int32(1)
        for m in range(at["seqs"]):
            size = lengths[order[m]]
            inside = begin <= block
            first = jnp.where(inside, begin, first)
            span = jnp.where(inside, size, span)
            begin = begin + size
        row = x_of * per + near
        draws = []
        for n in range(SLOTS - 5):
            spot = row * (SLOTS - 5) + n
            draw = jnp.where(far >= 2, rand_got[0, spot], rand_own[0, spot])
            for power in range(16, -1, -1):
                multiple = span * (1 << power)
                draw = jnp.where(draw >= multiple, draw - multiple, draw)
            draws.append(first + draw)
        candidates = [block - 1, block, block + 1, first, first + span - 1] + draws
        kept = []
        for s in range(SLOTS):
            alive = jnp.int32(1)
            if s == 0:
                alive = (block > first).astype(jnp.int32)
            if s == 2:
                alive = (block < first + span - 1).astype(jnp.int32)
            for e in range(s):
                same = (candidates[e] == candidates[s]).astype(jnp.int32)
                alive = alive * (1 - kept[e] * same)
            kept.append(alive)
            key = jnp.where(alive > 0, candidates[s], block)
            rel = key // MAXB - plane + 1
            inner = key % MAXB
            y_key, rest = inner // (4 * per), inner % (4 * per)
            core_key, rest = rest // (2 * per), rest % (2 * per)
            x_key, near_key = rest // per, rest % per
            spot = (rel * 2 + (core_key ^ core)) * 4 + ((y_key ^ y_at) * 2 + (x_key ^ x_at))
            idx_ref[i * SLOTS + s] = jnp.clip(spot * per + near_key, 0, 24 * per - 1)
            live_ref[i * SLOTS + s] = alive
        return carry

    lax.fori_loop(0, 4 * per, one, 0)


def attend_block(i, idx_ref, live_ref, q_ref, kv, lse_ref):
    qexp = spread_heads(q_ref[pl.ds(pl.multiple_of(i * BLK, BLK), BLK), :], 0)
    at = [idx_ref[i * SLOTS + s] for s in range(SLOTS)]
    off = [jnp.where(live_ref[i * SLOTS + s] > 0, 0.0, -NEG) for s in range(SLOTS)]
    keys = jnp.concatenate([kv[r, :, 0:WIN] for r in at], axis=0)
    values = jnp.concatenate([kv[r, :, 128 : 128 + WIN] for r in at], axis=0)
    raw = nt(keys, qexp)
    parts = [raw[s * BLK : (s + 1) * BLK] for s in range(SLOTS)]
    top = jnp.max(parts[1], axis=0, keepdims=True)
    for s in range(SLOTS):
        top = jnp.maximum(top, jnp.max(parts[s], axis=0, keepdims=True) - off[s])
    e = [jnp.exp(parts[s] - (top + off[s])) for s in range(SLOTS)]
    total = jnp.sum(e[0], axis=0, keepdims=True)
    for s in range(1, SLOTS):
        total = total + jnp.sum(e[s], axis=0, keepdims=True)
    lse_ref[pl.ds(i, 1), :] = top + jnp.log(total)
    scale = 1.0 / total
    probs = jnp.concatenate([(v * scale).astype(jnp.bfloat16) for v in e], axis=0)
    return fold_heads(tn(probs, values), 64).astype(jnp.bfloat16)


def forward_kernel(planes, tok_ref, wq_ref, wkv_ref, len_ref, ord_ref, rand_vm, rand_sm, *refs):
    kv_out, q_ref, x_out, ctx_out, lse_ref, idx_ref, live_ref = refs[:7]
    xs, kv, ctx, rand_got, rand_two = refs[7:12]
    x_send, x_recv, k_send, k_recv, up_send, up_recv, dn_send, dn_recv = refs[12:20]
    f_send, f_recv, g_send, g_recv, s_sem, o_send, o_recv, r_send, r_recv, l_sem = refs[20:30]
    plane, y_at, core, x_at = place()
    piece = tok_ref.shape[0]
    rows = piece // 2
    part = 4 * piece
    by_x = device_at(plane, y_at, core, 1 - x_at)
    by_y = device_at(plane, 1 - y_at, core, x_at)
    by_xy = device_at(plane, 1 - y_at, core, 1 - x_at)
    by_core = device_at(plane, y_at, 1 - core, x_at)
    above = device_at(plane + 1, y_at, core, x_at)
    below = device_at(plane - 1, y_at, core, x_at)
    has_above, has_below = plane < planes - 1, plane > 0
    ring = [device_at(lax.rem(plane + g, planes), y_at, core, x_at) for g in (1, planes - 1)]
    greet([by_x, by_y, by_xy, by_core] + ring)

    def x_rows(c):
        return xs.at[pl.ds((c - 2) * rows, rows)]

    def tok_rows(c):
        return tok_ref.at[pl.ds(c * rows, rows)]

    hops = {
        2: remote(tok_rows(0), x_rows(2), x_send, x_recv, 0, by_x),
        4: remote(tok_rows(0), x_rows(4), x_send, x_recv, 2, by_y),
        3: remote(tok_rows(1), x_rows(3), x_send, x_recv, 1, by_x),
        5: remote(tok_rows(1), x_rows(5), x_send, x_recv, 3, by_y),
        6: remote(x_rows(2), x_rows(6), x_send, x_recv, 4, by_y),
        7: remote(x_rows(5), x_rows(7), x_send, x_recv, 5, by_x),
    }
    rand_trade = remote(rand_vm, rand_got, r_send, r_recv, 0, by_y)
    rand_trade.start()
    for c in (2, 4, 3, 5):
        hops[c].start()

    def kv_rows(part_at, c):
        return kv.at[pl.ds((part_at * part + c * rows) // BLK, rows // BLK)]

    to_core, to_above, to_below, pass_up, pass_down = {}, {}, {}, {}, {}
    for c in range(8):
        mine = kv_rows(2, c)
        to_core[c] = remote(mine, kv_rows(3, c), k_send, k_recv, c, by_core)
        to_above[c] = remote(mine, kv_rows(0, c), up_send, up_recv, c, above)
        to_below[c] = remote(mine, kv_rows(4, c), dn_send, dn_recv, c, below)
        pass_up[c] = remote(kv_rows(0, c), kv_rows(1, c), f_send, f_recv, c, by_core)
        pass_down[c] = remote(kv_rows(4, c), kv_rows(5, c), g_send, g_recv, c, by_core)
    keeps = {
        c: pltpu.make_async_copy(
            tok_rows(c) if c < 2 else x_rows(c), x_out.at[pl.ds(c * rows, rows)], s_sem.at[c]
        )
        for c in range(8)
    }

    def relay(c):
        @pl.when(has_below)
        def _():
            to_above[c].wait_recv()
            pass_up[c].start()

        @pl.when(has_above)
        def _():
            to_below[c].wait_recv()
            pass_down[c].start()

    for n, c in enumerate(CHUNK_ORDER):
        if n == 2:
            rand_trade.wait()
            to_scalar = pltpu.make_async_copy(rand_got, rand_two, l_sem.at[0])
            to_scalar.start()
            to_scalar.wait()
            slot_tables(
                plane,
                y_at,
                core,
                x_at,
                dict(piece_blocks=piece // BLK, seqs=len_ref.shape[0]),
                len_ref,
                ord_ref,
                rand_sm,
                rand_two,
                idx_ref,
                live_ref,
            )
        if c >= 2:
            hops[c].wait_recv()
        if c == 2:
            hops[6].start()
        if c == 5:
            hops[7].start()
        keeps[c].start()
        block = tok_ref[pl.ds(c * rows, rows), :] if c < 2 else xs[pl.ds((c - 2) * rows, rows), :]
        made = jnp.dot(block, wkv_ref[...], preferred_element_type=jnp.float32).astype(jnp.bfloat16)
        kv[pl.ds((2 * part + c * rows) // BLK, rows // BLK)] = made.reshape(rows // BLK, BLK, -1)

        @pl.when(has_above)
        def _(c=c):
            to_above[c].start()

        @pl.when(has_below)
        def _(c=c):
            to_below[c].start()

        to_core[c].start()
        q_ref[pl.ds(c * rows, rows), :] = jnp.dot(
            block, wq_ref[...], preferred_element_type=jnp.float32
        ).astype(jnp.bfloat16)
        if n >= 3:
            relay(CHUNK_ORDER[n - 3])
    for c in CHUNK_ORDER[5:]:
        relay(c)
    for c in range(8):
        to_core[c].wait_recv()

        @pl.when(has_above)
        def _(c=c):
            pass_down[c].wait_recv()

        @pl.when(has_below)
        def _(c=c):
            pass_up[c].wait_recv()

    saved = pltpu.make_async_copy(kv, kv_out, l_sem.at[1])
    saved.start()
    per = piece // BLK
    trades = {}
    for j in JORDER:

        def step(n, carry, j=j):
            done = attend_block(j * per + n, idx_ref, live_ref, q_ref, kv, lse_ref)
            at = pl.ds(pl.multiple_of(n * BLK, BLK), BLK)
            if j:
                ctx[j - 1, at, :] = done
            else:
                ctx_out[at, 0:WIN] = done
            return carry

        lax.fori_loop(0, per, step, 0, unroll=2)
        if j:
            trades[j] = remote(
                ctx.at[j - 1],
                ctx_out.at[:, pl.ds(j * WIN, WIN)],
                o_send,
                o_recv,
                j - 1,
                device_at(plane, y_at ^ (j >> 1), core, x_at ^ (j & 1)),
            )
            trades[j].start()
    for c in (2, 4, 3, 5, 6, 7):
        hops[c].wait_send()
    for c in range(8):
        to_core[c].wait_send()
        keeps[c].wait()

        @pl.when(has_above)
        def _(c=c):
            to_above[c].wait_send()
            pass_down[c].wait_send()

        @pl.when(has_below)
        def _(c=c):
            to_below[c].wait_send()
            pass_up[c].wait_send()

    saved.wait()
    for j in (3, 1, 2):
        trades[j].wait()


def forward_attention(tokens, wq_own, wkv_own, lengths, seq_order, rand_row, planes):
    piece, width = tokens.shape
    dma, low = pltpu.SemaphoreType.DMA, jnp.bfloat16
    sds = jax.ShapeDtypeStruct
    blocks = 4 * piece // BLK
    return pl.pallas_call(
        functools.partial(forward_kernel, planes),
        out_shape=[
            sds((24 * piece // BLK, BLK, 2 * WQ), low),
            sds((4 * piece, WIN), low),
            sds((4 * piece, width), low),
            sds((piece, 4 * WIN), low),
            sds((blocks, WQ), jnp.float32),
            sds((blocks * SLOTS,), jnp.int32),
            sds((blocks * SLOTS,), jnp.int32),
        ],
        in_specs=[VMEM] * 3 + [SMEM] * 2 + [VMEM, SMEM],
        out_specs=[ANY, VMEM, ANY, VMEM, VMEM, SMEM, SMEM],
        scratch_shapes=[
            pltpu.VMEM((3 * piece, width), low),
            pltpu.VMEM((24 * piece // BLK, BLK, 2 * WQ), low),
            pltpu.VMEM((3, piece, WIN), low),
            pltpu.VMEM(rand_row.shape, jnp.int32),
            pltpu.SMEM(rand_row.shape, jnp.int32),
            dma((6,)),
            dma((6,)),
        ]
        + [dma((8,))] * 11
        + [dma((3,))] * 2
        + [dma((1,))] * 2
        + [dma((2,))],
        compiler_params=pltpu.CompilerParams(
            collective_id=0, has_side_effects=True, vmem_limit_bytes=62 << 20
        ),
        cost_estimate=pl.CostEstimate(
            flops=2 * 4 * piece * width * 640, bytes_accessed=40 << 20, transcendentals=0
        ),
        name="forward_attention",
    )(tokens, wq_own, wkv_own, lengths, seq_order, rand_row, rand_row)


def attend_back(idx, live, queries, grads, level, keys_values):
    rows, width = keys_values.shape[0] // 6, keys_values.shape[1]
    count = queries.shape[0]
    kv_shape = jax.ShapeDtypeStruct((6 * rows, width), jnp.bfloat16)
    return pl.pallas_call(
        backward_kernel,
        out_shape=[jax.ShapeDtypeStruct((count, WIN), jnp.bfloat16)] + [kv_shape],
        in_specs=[SMEM, SMEM, VMEM, VMEM, VMEM, ANY],
        out_specs=[VMEM] * 2,
        scratch_shapes=[
            pltpu.VMEM((6 * rows, width), jnp.bfloat16),
            pltpu.VMEM((6 * rows, width), jnp.float32),
            pltpu.SemaphoreType.DMA((1,)),
        ],
        compiler_params=pltpu.CompilerParams(vmem_limit_bytes=56 << 20),
        cost_estimate=pl.CostEstimate(
            flops=2 * 10 * count * 3 * 256 * 512, bytes_accessed=24 * rows * width, transcendentals=count * 3 * 512
        ),
        name="attend_back",
    )(idx, live, queries, grads, level, keys_values)


def reduce_kernel(planes, *refs):
    dkv_in, dq_in, x_in, wq_in, wkv_in, one_in = refs[:6]
    pair_in = refs[6:12]
    tok_out, q_out, k_out, v_out, up_out, side_out, norm_out, down_out = refs[12:20]
    own, core_in, z_out, z_in, g_all, dx_out, dx_in, acc = refs[20:28]
    dq, xs, wq, wkv, one = refs[28:33]
    p_slab, p_core, p_z, p_zin, p_fin, p_all = refs[33:39]
    keep, give = refs[39:42], refs[42:45]
    got, two, fin = refs[45:48], refs[48:51], refs[51:54]
    line_out, line_in = refs[54:57], refs[57:60]
    l_sem, i_sem, c_s, c_r, u_s, u_r, d_s, d_r, x_s, x_r = refs[60:70]
    pk_s, pk_r, pz_s, pz_r, pf_s, pf_r = refs[70:76]
    w2_s, w2_r, w3_s, w3_r, w4_s, w4_r = refs[76:82]
    plane, y_at, core, x_at = place()
    piece = tok_out.shape[0]
    part = 4 * piece
    rest = planes - 1
    group = y_at * 2 + x_at
    low, f32 = jnp.bfloat16, jnp.float32

    def there(j):
        return device_at(plane, y_at ^ (j >> 1), core, x_at ^ (j & 1))

    by_x, by_y = there(1), there(2)
    by_core = device_at(plane, y_at, 1 - core, x_at)
    others = [device_at(lax.rem(plane + g, planes), y_at, core, x_at) for g in range(1, planes)]
    has_above, has_below = plane < planes - 1, plane > 0
    above = device_at(plane + 1, y_at, core, x_at)
    below = device_at(plane - 1, y_at, core, x_at)

    def chunk(base, j):
        return pl.ds(pl.multiple_of(base + j * piece, piece), piece)

    def load_own(turn, r, j):
        return pltpu.make_async_copy(
            dkv_in.at[chunk(2 * r * part, j)], own.at[chunk(r * part, j)], l_sem.at[turn]
        )

    def to_core(turn, r, j):
        return remote(
            dkv_in.at[chunk((2 * r + 1) * part, j)],
            core_in.at[chunk(r * part, j)],
            c_s,
            c_r,
            turn,
            by_core,
        )

    def to_below(j):
        return remote(z_out.at[chunk(0, j)], z_in.at[chunk(0, j)], d_s, d_r, j, below)

    def to_above(j):
        return remote(z_out.at[chunk(part, j)], z_in.at[chunk(part, j)], u_s, u_r, j, above)

    def to_owner(j):
        return remote(dx_out.at[j - 1], dx_in.at[j - 1], x_s, x_r, j - 1, there(j))

    def every(n, action):
        j = 3 - n
        for turn, r in ((n * 2, 0), (n * 2 + 1, 2)):
            action(turn, r, j)

    greet([by_x, by_y, there(3), by_core] + others)

    def begin(n, carry):
        def go(turn, r, j):
            to_core(turn, r, j).start()
            load_own(turn, r, j).start()

        every(n, go)
        return carry

    lax.fori_loop(0, 4, begin, 0)

    def begin_mid(n, carry):
        to_core(8 + n, 1, 3 - n).start()
        load_own(8 + n, 1, 3 - n).start()
        return carry

    lax.fori_loop(0, 4, begin_mid, 0)
    inputs = [(pair_in[2 * n], keep[n]) for n in range(3)]
    inputs += [(pair_in[2 * n + 1], give[n]) for n in range(3)]
    inputs += [(wq_in, wq), (wkv_in, wkv), (dq_in, dq), (x_in, xs), (one_in, one)]
    inputs = [pltpu.make_async_copy(src, dst, i_sem.at[n]) for n, (src, dst) in enumerate(inputs)]
    for copy in inputs:
        copy.start()

    def both(turn, r, j):
        to_core(turn, r, j).wait_recv()
        load_own(turn, r, j).wait()
        at = chunk(r * part, j)
        return own[at, :].astype(f32) + core_in[at, :].astype(f32)

    def spread(n, carry):
        j = 3 - n
        z_out[chunk(0, j), :] = both(2 * n, 0, j).astype(low)

        @pl.when(has_below)
        def _():
            to_below(j).start()

        z_out[chunk(part, j), :] = both(2 * n + 1, 2, j).astype(low)

        @pl.when(has_above)
        def _():
            to_above(j).start()

        return carry

    lax.fori_loop(0, 4, spread, 0)

    for copy in inputs[:6]:
        copy.wait()
    halves = [keep[0].shape[2] // 2, keep[1].shape[2] // 2]
    w2 = []
    for n in range(3):

        def merge(p, carry, n=n):
            keep[n][p] = (keep[n][p].astype(f32) + give[n][p].astype(f32)).astype(low)
            return carry

        lax.fori_loop(0, planes, merge, 0)
        if n < 2:
            cols = pl.ds(pl.multiple_of((1 - x_at) * halves[n], 128), halves[n])
            w2.append(remote(keep[n].at[:, :, cols], got[n], w2_s, w2_r, n, by_x))
        else:
            w2.append(remote(keep[n].at[:, 1 - y_at], got[n], w2_s, w2_r, n, by_y))
        w2[n].start()
    for copy in inputs[6:]:
        copy.wait()
    acc[...] = jnp.zeros_like(acc)

    def arrive(n):
        j = 3 - n
        g_all[:, 2 * WQ :] = dq[chunk(0, j), :]
        g_all[:, : 2 * WQ] = both(8 + n, 1, j).astype(low)

        @pl.when(has_above)
        def _():
            to_below(j).wait_recv()
            g_all[:, : 2 * WQ] = (
                g_all[:, : 2 * WQ].astype(f32) + z_in[chunk(0, j), :].astype(f32)
            ).astype(low)

        @pl.when(has_below)
        def _():
            to_above(j).wait_recv()
            g_all[:, : 2 * WQ] = (
                g_all[:, : 2 * WQ].astype(f32) + z_in[chunk(part, j), :].astype(f32)
            ).astype(low)

    def back(j):
        grads = g_all[...]
        return nt(grads[:, 2 * WQ :], wq[...]) + nt(grads[:, : 2 * WQ], wkv[...])

    def outer(j):
        acc[...] += tn(xs[chunk(0, j), :], g_all[...])

    def send_back(n, carry):
        arrive(n)
        dx_out[2 - n] = back(3 - n).astype(low)
        to_owner(3 - n).start()
        outer(3 - n)
        return carry

    lax.fori_loop(0, 3, send_back, 0)

    for n in range(3):
        w2[n].wait_recv()

        def halve(p, carry, n=n):
            if n < 2:
                cols = pl.ds(pl.multiple_of(x_at * halves[n], 128), halves[n])
                mine = keep[n][p, :, cols]
            else:
                mine = keep[n][p, y_at]
            two[n][p] = (mine.astype(f32) + got[n][p].astype(f32)).astype(low)
            return carry

        lax.fori_loop(0, planes, halve, 0)

    def line_copy(n, way, t):
        return remote(
            line_out[n].at[way, t],
            line_in[n].at[way, t],
            w3_s,
            w3_r,
            (n * 2 + way) * rest + t,
            below if way else above,
        )

    def line_step(t):
        for n in range(3):
            for way in range(2):
                spot = (planes - 1 - plane) if way else plane
                gap = planes - 1 - t
                slab = (plane - gap) if way else (plane + gap)
                sends = jnp.logical_and(t >= spot, spot < planes - 1)

                @pl.when(jnp.logical_and(sends, spot == 0))
                def _():
                    line_out[n][way, t] = two[n][slab]
                    line_copy(n, way, t).start()

                @pl.when(jnp.logical_and(sends, spot > 0))
                def _():
                    line_copy(n, way, t - 1).wait_recv()
                    line_out[n][way, t] = (
                        two[n][slab].astype(f32) + line_in[n][way, t - 1].astype(f32)
                    ).astype(low)
                    line_copy(n, way, t).start()

    arrive(3)
    line_step(0)
    tok_out[...] = one[...] + back(0)
    outer(0)

    share = p_slab.shape[3]
    for p in range(planes):
        for y in range(2):
            for k in range(2):
                at = ((p * 2 + y) * 2 + k) * share
                p_slab[k, p, y] = acc[at : at + share, :].astype(low)
    pk = remote(p_slab.at[1 - core], p_core, pk_s, pk_r, 0, by_core)
    pk.start()
    if planes > 2:
        line_step(1)
    pk.wait_recv()

    def merge_core(p, carry):
        p_z[p] = (p_slab[core, p].astype(f32) + p_core[p].astype(f32)).astype(low)
        return carry

    lax.fori_loop(0, planes, merge_core, 0)
    pz = [
        remote(
            p_z.at[lax.rem(plane + g, planes)], p_zin.at[g - 1], pz_s, pz_r, g - 1, others[g - 1]
        )
        for g in range(1, planes)
    ]
    for copy in pz:
        copy.start()

    def next_step(t, carry):
        line_step(t)
        return carry

    lax.fori_loop(2, planes - 1, next_step, 0)
    for j in (3, 2, 1):
        to_owner(j).wait_recv()
        tok_out[...] += dx_in[j - 1].astype(f32)

    total = p_z[plane].astype(f32)
    for g in range(1, planes):
        pz[g - 1].wait_recv()
        total = total + p_zin[g - 1].astype(f32)
    p_fin[...] = total.astype(low)
    pf = [
        remote(p_fin.at[y_at ^ (j >> 1)], p_all.at[j], pf_s, pf_r, j - 1, there(j))
        for j in (1, 2, 3)
    ]
    for copy in pf:
        copy.start()
    p_all[0] = p_fin[y_at]

    w4 = []
    for n in range(3):
        fin[n][x_at] = two[n][plane]

        @pl.when(has_below)
        def _(n=n):
            line_copy(n, 0, rest - 1).wait_recv()
            fin[n][x_at] = (
                fin[n][x_at].astype(f32) + line_in[n][0, rest - 1].astype(f32)
            ).astype(low)

        @pl.when(has_above)
        def _(n=n):
            line_copy(n, 1, rest - 1).wait_recv()
            fin[n][x_at] = (
                fin[n][x_at].astype(f32) + line_in[n][1, rest - 1].astype(f32)
            ).astype(low)

        w4.append(remote(fin[n].at[x_at], fin[n].at[x_at], w4_s, w4_r, n, by_x))
        w4[n].start()

    for copy in pf:
        copy.wait()
    for a in range(4):
        grads = p_all[a ^ group].astype(f32)
        for n, dest in enumerate((k_out, v_out, q_out)):
            dest[:, a * WQ : (a + 1) * WQ] = grads[:, n * WQ : (n + 1) * WQ]
    for n, dest in ((0, up_out), (2, down_out)):
        w4[n].wait()
        width = dest.shape[1] // 2
        for side in range(2):
            dest[:, side * width : (side + 1) * width] = fin[n][side].astype(f32)
    w4[1].wait()
    width = side_out.shape[1] // 2
    for side in range(2):
        done = fin[1][side].astype(f32)
        side_out[:, side * width : (side + 1) * width] = done[:share]
        norm_out[:, side * width : (side + 1) * width] = done[share : share + 8]

    for copy in w2 + pz + [pk]:
        copy.wait_send()

    def settle(n, carry):
        every(n, lambda turn, r, j: to_core(turn, r, j).wait_send())
        to_core(8 + n, 1, 3 - n).wait_send()

        @pl.when(has_below)
        def _():
            to_below(3 - n).wait_send()

        @pl.when(has_above)
        def _():
            to_above(3 - n).wait_send()

        return carry

    lax.fori_loop(0, 4, settle, 0)
    for j in (1, 2, 3):
        to_owner(j).wait_send()

    def settle_line(t, carry):
        for n in range(3):
            for way in range(2):
                spot = (planes - 1 - plane) if way else plane

                @pl.when(jnp.logical_and(t >= spot, spot < planes - 1))
                def _():
                    line_copy(n, way, t).wait_send()

        return carry

    lax.fori_loop(0, planes - 1, settle_line, 0)


def reduce_all(dkv, dq, stretch, wq, wkv, one, up, out, down, planes):
    low, f32 = jnp.bfloat16, jnp.float32
    piece = dq.shape[0] // 4
    width = stretch.shape[1]
    share = up[0].shape[1]
    rest = planes - 1
    dma, vm, sds = pltpu.SemaphoreType.DMA, pltpu.VMEM, jax.ShapeDtypeStruct
    cols = 2 * WQ + WIN
    tall = out[0].shape[1]
    wide = up[0].shape[2]
    kinds = [(share, wide // 2), (tall, width // 2), down[0].shape[2:]]
    pairs = [up[0].shape, out[0].shape, down[0].shape]
    return pl.pallas_call(
        functools.partial(reduce_kernel, planes),
        out_shape=[sds((piece, width), f32)]
        + [sds((share, width), f32)] * 3
        + [
            sds((share, wide), f32),
            sds((share, width), f32),
            sds((8, width), f32),
            sds((kinds[2][0], width), f32),
        ],
        in_specs=[ANY] * 12,
        out_specs=[VMEM] * 8,
        scratch_shapes=[
            vm((12 * piece, 2 * WQ), low),
            vm((12 * piece, 2 * WQ), low),
            vm((8 * piece, 2 * WQ), low),
            vm((8 * piece, 2 * WQ), low),
            vm((piece, cols), low),
            vm((3, piece, width), low),
            vm((3, piece, width), low),
            vm((width, cols), f32),
            vm(dq.shape, low),
            vm(stretch.shape, low),
            vm(wq.shape, low),
            vm(wkv.shape, low),
            vm(one.shape, f32),
            vm((2, planes, 2, share, cols), low),
            vm((planes, 2, share, cols), low),
            vm((planes, 2, share, cols), low),
            vm((rest, 2, share, cols), low),
            vm((2, share, cols), low),
            vm((4, share, cols), low),
        ]
        + [vm(p, low) for p in pairs] * 2
        + [vm((planes,) + k, low) for k in kinds] * 2
        + [vm((2,) + k, low) for k in kinds]
        + [vm((2, rest) + k, low) for k in kinds] * 2
        + [dma((12,)), dma((11,))]
        + [dma((12,))] * 2
        + [dma((4,))] * 4
        + [dma((3,))] * 2
        + [dma((1,))] * 2
        + [dma((rest,))] * 2
        + [dma((3,))] * 2
        + [dma((3,))] * 2
        + [dma((6 * rest,))] * 2
        + [dma((3,))] * 2,
        compiler_params=pltpu.CompilerParams(
            collective_id=1, has_side_effects=True, vmem_limit_bytes=60 << 20
        ),
        cost_estimate=pl.CostEstimate(
            flops=4 * 4 * piece * width * cols, bytes_accessed=40 << 20, transcendentals=0
        ),
        name="reduce_all",
    )(dkv, dq, stretch, wq, wkv, one, up[0], up[1], out[0], out[1], down[0], down[1])


def dense_kernel(
    planes,
    tok_ref,
    ctx_ref,
    cot_ref,
    g1_ref,
    b1_ref,
    g2_ref,
    b2_ref,
    wout_ref,
    wup_in,
    wdown_in,
    *refs,
):
    out_ref, one_ref, do_out, up_keep, up_give, out_keep, out_give, down_keep, down_give = refs[:9]
    wup, wdown, acc, x1, s1, g_two, nl, hid, slope, gp, gm, ga = refs[9:21]
    dctx, up_loc, out_loc, down_loc, up_got, out_got, down_got, down_sum = refs[21:29]
    w_sem, mv_sem, do_s, do_r, up_s, up_r, out_s, out_r, down_s, down_r = refs[29:39]
    plane, y_at, core, x_at = place()
    piece, width = tok_ref.shape
    share = up_loc.shape[2]
    slab = down_loc.shape[2]
    pairs = 2 * planes
    group = y_at * 2 + x_at
    f32 = jnp.float32
    bring = [
        pltpu.make_async_copy(wup_in, wup, w_sem.at[0]),
        pltpu.make_async_copy(wdown_in, wdown, w_sem.at[1]),
    ]
    for copy in bring:
        copy.start()

    def there(j):
        return device_at(plane, y_at ^ (j >> 1), core, x_at ^ (j & 1))

    by_core = device_at(plane, y_at, 1 - core, x_at)
    greet([there(1), there(2), there(3), by_core])

    height, tile = 32, 2 * WQ
    wide = wup.shape[1]

    def rows_of(n):
        return pl.ds(pl.multiple_of(n * height, height), height)

    def cols_of(n):
        return pl.ds(pl.multiple_of(n * tile, tile), tile)

    def mean(v):
        return jnp.mean(v, axis=1, keepdims=True)

    def fold(v):
        return v[:8] + v[8:16] + v[16:24] + v[24:]

    acc[...] = jnp.dot(ctx_ref[...], wout_ref[...], preferred_element_type=f32)
    g1, b1, g2, b2 = (r[...].reshape(1, width) for r in (g1_ref, b1_ref, g2_ref, b2_ref))

    def norm_one(n, carry):
        at = rows_of(n)
        value = tok_ref[at, :].astype(f32) + acc[at, :]
        center = value - mean(value)
        inverse = lax.rsqrt(mean(center * center) + eps_norm)
        hat = center * inverse
        x1[at, :] = hat
        s1[at, :] = jnp.broadcast_to(inverse, (height, 128))
        nl[at, :] = (hat * g1 + b1).astype(jnp.bfloat16)
        return carry

    lax.fori_loop(0, piece // height, norm_one, 0, unroll=2)
    bring[0].wait()

    def expand(n, carry):
        at = cols_of(n)
        pre = jnp.dot(nl[...], wup[:, at], preferred_element_type=f32)
        square = pre * pre
        inner = 0.7978845608028654 * pre * (1.0 + 0.044715 * square)
        bend = jnp.tanh(inner)
        half_up = 0.5 + 0.5 * bend
        hid[:, at] = (pre * half_up).astype(jnp.bfloat16)
        slope[:, at] = half_up + 0.5 * pre * (1.0 - bend * bend) * (
            0.7978845608028654 + 0.1070322243 * square
        )
        return carry

    lax.fori_loop(0, wide // tile, expand, 0)
    bring[1].wait()
    acc[...] = jnp.dot(hid[...], wdown[...], preferred_element_type=f32)
    nothing = jnp.zeros((8, width), f32)

    def norm_two(n, carry):
        gain_sum, shift_sum = carry
        at = rows_of(n)
        value = x1[at, :] * g1 + b1 + acc[at, :]
        center = value - mean(value)
        inverse = lax.rsqrt(mean(center * center) + eps_norm)
        hat = center * inverse
        out_ref[at, :] = (hat * g2 + b2).astype(jnp.bfloat16)
        cot = cot_ref[at, :].astype(f32)
        gain_sum, shift_sum = gain_sum + fold(cot * hat), shift_sum + fold(cot)
        up = cot * g2
        grad = inverse * (up - mean(up) - hat * mean(up * hat))
        g_two[at, :] = grad
        gm[at, :] = grad.astype(jnp.bfloat16)
        return gain_sum, shift_sum

    gain_two, shift_two = lax.fori_loop(0, piece // height, norm_two, (nothing, nothing), unroll=2)

    def shrink(n, carry):
        at = cols_of(n)
        back = nt(gm[...], wdown[at, :])
        gp[:, at] = (back * slope[:, at]).astype(jnp.bfloat16)
        return carry

    lax.fori_loop(0, wide // tile, shrink, 0)
    acc[...] = nt(gp[...], wup[...])

    def norm_three(n, carry):
        gain_sum, shift_sum = carry
        at = rows_of(n)
        grad_in, hat = g_two[at, :] + acc[at, :], x1[at, :]
        gain_sum, shift_sum = gain_sum + fold(grad_in * hat), shift_sum + fold(grad_in)
        up = grad_in * g1
        grad = s1[at, 0:1] * (up - mean(up) - hat * mean(up * hat))
        one_ref[at, :] = grad
        ga[at, :] = grad.astype(jnp.bfloat16)
        return gain_sum, shift_sum

    gain_one, shift_one = lax.fori_loop(
        0, piece // height, norm_three, (nothing, nothing), unroll=2
    )
    side = jnp.concatenate(
        [jnp.sum(v, axis=0, keepdims=True) for v in (gain_one, shift_one, gain_two, shift_two)]
        + [jnp.zeros((12, width), f32)],
        axis=0,
    ).astype(jnp.bfloat16)

    low = jnp.bfloat16
    trades = []
    for j in (3, 1, 2, 0):
        part = nt(ga[...], wout_ref[pl.ds(j * WIN, WIN), :]).astype(low)
        if j:
            dctx[j - 1] = part
            trades.append(
                remote(
                    dctx.at[j - 1], do_out.at[pl.ds(j * piece, piece)], do_s, do_r, j - 1, there(j)
                )
            )
            trades[-1].start()
        else:
            do_out[pl.ds(0, piece), :] = part

    to_core = []
    tile = 2 * WQ
    per = tile // (2 * slab)
    for t in range(hid.shape[1] // tile):
        cell = tn(hid[:, t * tile : (t + 1) * tile], gm[...])
        for n in range(per):
            for k in range(2):
                at = (n * 2 + k) * slab
                down_loc[k, t * per + n] = cell[at : at + slab].astype(low)
        span = pl.ds(t * per, per)
        to_core.append(
            remote(down_loc.at[1 - core, span], down_got.at[span], down_s, down_r, t, by_core)
        )
        to_core[-1].start()
    ups = []
    for t in range(gp.shape[1] // tile):
        span = pl.ds(t * tile, tile)
        cell = tn(nl[...], gp[:, t * tile : (t + 1) * tile])
        for q in range(pairs):
            for k in range(2):
                at = (q * 2 + k) * share
                up_loc[k, q, :, t * tile : (t + 1) * tile] = cell[at : at + share].astype(low)
        ups.append(
            remote(
                up_loc.at[1 - core, :, :, span], up_got.at[:, :, span], up_s, up_r, t, by_core
            )
        )
        ups[-1].start()
    per_group = pairs // 4
    for j in range(4):
        cell = tn(ctx_ref[:, j * WIN : (j + 1) * WIN], ga[...])
        for n in range(per_group):
            for k in range(2):
                at = WIN - WQ + (n * 2 + k) * share
                out_loc[k, (group ^ j) * per_group + n, :share, :] = cell[at : at + share].astype(low)
    for q in range(pairs):
        for k in range(2):
            out_loc[k, q, share:, :] = side
    outs = remote(out_loc.at[1 - core], out_got, out_s, out_r, 0, by_core)
    outs.start()

    moved = []

    def move(source, dest):
        moved.append(pltpu.make_async_copy(source, dest, mv_sem.at[len(moved)]))
        moved[-1].start()

    half = width // 2
    for n, copy in enumerate(to_core):
        copy.wait_recv()
        for q in range(n * per, (n + 1) * per):
            total = (
                down_loc[core, q].astype(jnp.float32) + down_got[q].astype(jnp.float32)
            ).astype(low)
            down_sum[0, q] = total[:, :half]
            down_sum[1, q] = total[:, half:]
    move(down_sum.at[x_at], down_keep)
    move(down_sum.at[1 - x_at], down_give)
    for copy in ups:
        copy.wait_recv()
    for p in range(planes):
        for y in range(2):
            q = p * 2 + y
            up_got[q] = (up_loc[core, q].astype(jnp.float32) + up_got[q].astype(jnp.float32)).astype(low)
    outs.wait_recv()
    for p in range(planes):
        for y in range(2):
            q = p * 2 + y
            out_got[q] = (
                out_loc[core, q].astype(jnp.float32) + out_got[q].astype(jnp.float32)
            ).astype(low)
        for got, keep, give in ((up_got, up_keep, up_give), (out_got, out_keep, out_give)):
            move(got.at[p * 2 + y_at], keep.at[p])
            move(got.at[p * 2 + 1 - y_at], give.at[p])
    for copy in trades:
        copy.wait()
    for copy in to_core + ups + [outs]:
        copy.wait_send()
    for copy in moved:
        copy.wait()


def dense_layers(tokens, ctx, cotangent, norms, wout, w_up, w_down, planes):
    low = jnp.bfloat16
    piece, width = tokens.shape
    pairs = 2 * planes
    wide = w_up.shape[1]
    share, slab, tall = width // (2 * pairs), wide // (2 * pairs), 16
    sds, vm, dma = jax.ShapeDtypeStruct, pltpu.VMEM, pltpu.SemaphoreType.DMA
    up, out = (planes, share, wide), (planes, share + tall, width)
    down = (pairs, slab, width // 2)
    tiles = wide // (2 * WQ)
    f32 = jnp.float32
    return pl.pallas_call(
        functools.partial(dense_kernel, planes),
        out_shape=[sds((piece, width), low), sds((piece, width), f32), sds((4 * piece, WIN), low)]
        + [sds(up, low)] * 2
        + [sds(out, low)] * 2
        + [sds(down, low)] * 2,
        in_specs=[VMEM] * 8 + [ANY] * 2,
        out_specs=[VMEM] * 3 + [ANY] * 6,
        scratch_shapes=[
            vm(w_up.shape, low),
            vm(w_down.shape, low),
            vm((piece, width), f32),
            vm((piece, width), f32),
            vm((piece, 128), f32),
            vm((piece, width), f32),
            vm((piece, width), low),
            vm((piece, wide), low),
            vm((piece, wide), f32),
            vm((piece, wide), low),
            vm((piece, width), low),
            vm((piece, width), low),
            vm((3, piece, WIN), low),
            vm((2, pairs, share, wide), low),
            vm((2, pairs, share + tall, width), low),
            vm((2, pairs, slab, width), low),
            vm((pairs, share, wide), low),
            vm((pairs, share + tall, width), low),
            vm((pairs, slab, width), low),
            vm((2, pairs, slab, width // 2), low),
            dma((2,)),
            dma((2 + 4 * planes,)),
        ]
        + [dma((3,))] * 2
        + [dma((tiles,))] * 2
        + [dma((1,))] * 2
        + [dma((tiles,))] * 2,
        compiler_params=pltpu.CompilerParams(
            collective_id=2, has_side_effects=True, vmem_limit_bytes=62 << 20
        ),
        cost_estimate=pl.CostEstimate(
            flops=2 * piece * width * (6 * wide + 3072), bytes_accessed=30 << 20, transcendentals=0
        ),
        name="dense_layers",
    )(tokens, ctx, cotangent, *norms, wout, w_up, w_down)


def pick(array, at, axis):
    return lax.dynamic_index_in_dim(array, at, axis, keepdims=False)


def body(
    tokens,
    w_query,
    w_key,
    w_value,
    w_out,
    gain_attn,
    shift_attn,
    w_up,
    w_down,
    gain_mlp,
    shift_mlp,
    cotangent,
    lengths,
    seq_order,
    rand_blocks,
):
    piece, width = tokens.shape
    seqs, heads = lax.axis_size("seq"), lax.axis_size("head")
    planes = seqs // 4
    assert heads == 2 and 8 * piece == MAXB * BLK and width == 4 * WQ
    seq_at, x_at = lax.axis_index("seq"), lax.axis_index("head")
    plane, y_at, core = seq_at // 4, (seq_at // 2) % 2, seq_at % 2
    group = y_at * 2 + x_at

    def columns(weights):
        return lax.dynamic_slice_in_dim(weights, group * WQ, WQ, 1)

    wq_own = jnp.pad(columns(w_query) * jnp.bfloat16(DH ** (-0.5)), ((0, 0), (0, WIN - WQ)))
    wkv_own = jnp.concatenate([columns(w_key), columns(w_value)], axis=1)
    order = [group ^ j for j in range(4)]
    wout_own = jnp.concatenate(
        [
            jnp.pad(lax.dynamic_slice_in_dim(w_out, g * WQ, WQ, 0), ((WIN - WQ, 0), (0, 0)))
            for g in order
        ],
        axis=0,
    )

    flat = rand_blocks.reshape(1, -1)
    rand_row = jnp.pad(flat, ((0, 0), (0, 128 - flat.shape[1])))
    keys_values, queries, stretch, context_tok, level, idx, live = forward_attention(
        tokens, wq_own, wkv_own, lengths, seq_order, rand_row, planes
    )
    share = width // seqs
    norms = [gain_attn, shift_attn, gain_mlp, shift_mlp]
    output, grad_one, grad_ctx, up_keep, up_give, out_keep, out_give, down_keep, down_give = (
        dense_layers(tokens, context_tok, cotangent, norms, wout_own, w_up, w_down, planes)
    )
    up_pair = (up_keep, xor_swap(up_give, 4))
    out_pair = (out_keep, xor_swap(out_give, 4))
    two_y = (planes, 2) + down_keep.shape[1:]
    down_pair = (down_keep.reshape(two_y), xor_swap(down_give, 1).reshape(two_y))

    grad_q, grad_kv = attend_back(
        idx, live, queries, grad_ctx, level, keys_values.reshape(-1, 2 * WQ)
    )
    wq_plain = jnp.pad(columns(w_query), ((0, 0), (0, WIN - WQ)))
    grad_tokens, grad_wq, grad_wk, grad_wv, up_total, out_total, norm_rows, down_total = reduce_all(
        grad_kv,
        grad_q,
        stretch,
        wq_plain,
        wkv_own,
        grad_one,
        up_pair,
        out_pair,
        down_pair,
        planes,
    )

    def norm_grad(n):
        return lax.dynamic_slice_in_dim(norm_rows[n], seq_at * share, share, 0)

    return (
        output,
        grad_tokens,
        grad_wq,
        grad_wk,
        grad_wv,
        out_total,
        norm_grad(0),
        norm_grad(1),
        up_total,
        down_total,
        norm_grad(2),
        norm_grad(3),
    )


def solution(mesh):
    rows = P(("seq", "head"), None)
    seq_rows, seq_only = P("seq", None), P("seq")
    return jax.shard_map(
        body,
        mesh=mesh,
        in_specs=(rows,) + (P(),) * 10 + (rows, P(), P(), seq_rows),
        out_specs=(
            rows,
            rows,
            seq_rows,
            seq_rows,
            seq_rows,
            seq_rows,
            seq_only,
            seq_only,
            seq_rows,
            seq_rows,
            seq_only,
            seq_only,
        ),
        check_vma=False,
    )
```

profile of v0, /device:TPU:24, one launch (start us, length us, event | category | flops | bytes accessed | tf_op | source)
XLA Modules:
  0.0 249.1 jit_solution(14793710569003839249)
XLA Ops:
  0.7 0.8 copy.28
  2.3 1.7 broadcast_multiply_fusion
  4.0 0.8 pad.24.wq_ref
  4.8 1.0 pad_maximum_fusion.wkv_ref.refs_4_
  6.0 1.2 fusion.7.wout_ref
  7.2 67.6 %forward_attention.1 = (bf16[192,64,384]{2,1,0:T(8,128)(2,1)}, bf16[2048,256]{1,0:T(8,128)(2,1)}, bf16[2048,768]{1,0:T(8,128)(2,1)}, bf16[512,1024]{1,0:T(8,128)...) custom-call(bf16[512,768]{1,0:T(8,128)(2,1)} %tok_ref.3, bf16[768,256]{1,0:T(8,128)(2,1)} %pad.24.wq_ref, ...), custom_call_target="tpu_custom_call" | custom-call | flops 2013265920 | bytes 41943040 | tf_op jit(solution)/shard_map/forward_attention/pallas_call | solution.py:396
  74.8 47.1 %dense_layers.1 = (bf16[512,768]{1,0:T(8,128)(2,1)}, f32[512,768]{1,0:T(8,128)}, bf16[2048,256]{1,0:T(8,128)(2,1)}, bf16[4,48,3072]{2,1,0:T(8,128)(2,1)}, bf16[4...) custom-call(bf16[512,768]{1,0:T(8,128)(2,1)} %tok_ref.3, ...), custom_call_target="tpu_custom_call" | custom-call | flops 16911433728 | bytes 31457280 | tf_op jit(solution)/shard_map/dense_layers/pallas_call | solution.py:1105
  121.8 0.8 collective-permute-start.1
  122.6 1.3 collective-permute-start
  123.9 0.7 collective-permute-start.2
  124.6 29.2 %attend_back.1 = (bf16[2048,256]{1,0:T(8,128)(2,1)}, bf16[12288,384]{1,0:T(8,128)(2,1)}) custom-call(s32[256]{0:T(256)} %get-tuple-element.40.idx_ref, s32[256]{0:T(256)} %get-tuple-element.41.live_ref, bf16[2048,256]{1,0:T(8,128)(2,1)} %get-tuple-element.42.q_ref, bf16[2048,256]{1,0:T(8,128)(2,1)} %get-tuple-element.43.do_ref, ...), custom_call_target="tpu_custom_call" | custom-call | flops 16106127360 | bytes 18874368 | tf_op jit(solution)/shard_map/attend_back/pallas_call | solution.py:436
  153.8 0.8 pad.30.refs_3_
  154.7 4.1 %collective-permute-done.refs_7_ = bf16[4,48,3072]{2,1,0:T(8,128)(2,1)S(1)} collective-permute-done((bf16[4,48,3072]{2,1,0:T(8,128)(2,1)}, bf16[4,48,3072]{2,1,0:T(8,128)(2,1)S(1)}, u32[]{:S(2)}, u32[]{:S(2)}) %collective-permute-start) | collective-permute-done | bytes 1179680 | tf_op jit(solution)/shard_map/ppermute | solution.py:25
  158.8 1.0 copy-done.3
  159.8 79.7 %reduce_all.1 = (f32[512,768]{1,0:T(8,128)}, f32[48,768]{1,0:T(8,128)}, f32[48,768]{1,0:T(8,128)}, f32[48,768]{1,0:T(8,128)}, f32[48,3072]{1,0:T(8,128)}, /*inde...) custom-call(bf16[12288,384]{1,0:T(8,128)(2,1)} %get-tuple-element.46.refs_0_, ...), custom_call_target="tpu_custom_call" | custom-call | flops 4026531840 | bytes 41943040 | tf_op jit(solution)/shard_map/reduce_all/pallas_call | solution.py:805
  239.5 0.9 fusion.13
  242.7 0.9 copy.37
  243.6 1.1 copy.38
  244.8 0.7 copy.39
  245.4 0.7 copy.40
  246.1 0.7 copy.41
  246.8 0.7 copy.42
  247.4 0.8 copy.43
  248.3 0.8 copy.44
  (33 shorter events, 3.3 us)
Async XLA Ops:
  0.6 1.5 copy-start
  4.0 1.9 copy-start.2
  121.8 32.8 %collective-permute-start.1 = (bf16[4,64,768]{2,1,0:T(8,128)(2,1)}, bf16[4,64,768]{2,1,0:T(8,128)(2,1)S(1)}, u32[]{:S(2)}, u32[]{:S(2)}) collective-permute-start(bf16[4,64,768]{2,1,0:T(8,128)(2,1)} %get-tuple-element.53), channel_id=1, source_target_pairs={{0,4},{1,5},{2,6},{3,7},{4,0},{5,1},{6,2},{7,3},{8,12},{9,13},{10,... | collective-permute-start | bytes 1179656 | tf_op jit(solution)/shard_map/ppermute | solution.py:25
  122.6 36.1 %collective-permute-start = (bf16[4,48,3072]{2,1,0:T(8,128)(2,1)}, bf16[4,48,3072]{2,1,0:T(8,128)(2,1)S(1)}, u32[]{:S(2)}, u32[]{:S(2)}) collective-permute-start(bf16[4,48,3072]{2,1,0:T(8,128)(2,1)} %get-tuple-element.51), channel_id=1, source_target_pairs={{0,4},{1,5},{2,6},{3,7},{4,0},{5,1},{6,2},{7,3},{8,12},{9,13},{10,... | collective-permute-start | bytes 3538952 | tf_op jit(solution)/shard_map/ppermute | solution.py:25
  123.9 34.8 %collective-permute-start.2 = (bf16[8,192,384]{2,1,0:T(8,128)(2,1)}, bf16[8,192,384]{2,1,0:T(8,128)(2,1)}, u32[]{:S(2)}, u32[]{:S(2)}) collective-permute-start(bf16[8,192,384]{2,1,0:T(8,128)(2,1)} %get-tuple-element.55), channel_id=1, source_target_pairs={{0,1},{1,0},{2,3},{3,2},{4,5},{5,4},{6,7},{7,6},{8,9},{9,8},{10,11... | collective-permute-start | bytes 3538952 | tf_op jit(solution)/shard_map/ppermute | solution.py:25
  154.7 4.1 %copy-start.7 = (bf16[4,64,768]{2,1,0:T(8,128)(2,1)}, bf16[4,64,768]{2,1,0:T(8,128)(2,1)S(1)}, u32[]{:S(2)}) copy-start(bf16[4,64,768]{2,1,0:T(8,128)(2,1)S(1)} %collective-permute-done.1.refs_9_) | copy-start | bytes 1179652
  158.7 1.0 copy-start.3
  159.8 83.0 %copy-start.4 = (bf16[512,768]{1,0:T(8,128)(2,1)S(1)}, bf16[512,768]{1,0:T(8,128)(2,1)}, u32[]{:S(2)}) copy-start(bf16[512,768]{1,0:T(8,128)(2,1)} %get-tuple-element.87) | copy-start | bytes 2359300
  239.4 4.1 %copy-start.1 = (f32[512,768]{1,0:T(8,128)S(1)}, f32[512,768]{1,0:T(8,128)}, u32[]{:S(2)}) copy-start(f32[512,768]{1,0:T(8,128)} %get-tuple-element.88) | copy-start | bytes 4718596
  243.6 1.2 copy-start.11
  243.6 1.8 copy-start.10
  243.6 2.5 %copy-start.9 = (f32[48,768]{1,0:T(8,128)S(1)}, f32[48,768]{1,0:T(8,128)}, u32[]{:S(2)}) copy-start(f32[48,768]{1,0:T(8,128)} %get-tuple-element.91) | copy-start | bytes 442372
  243.6 3.2 %copy-start.8 = (f32[48,768]{1,0:T(8,128)S(1)}, f32[48,768]{1,0:T(8,128)}, u32[]{:S(2)}) copy-start(f32[48,768]{1,0:T(8,128)} %get-tuple-element.92) | copy-start | bytes 442372
  243.6 3.8 %copy-start.6 = (f32[48,3072]{1,0:T(8,128)S(1)}, f32[48,3072]{1,0:T(8,128)}, u32[]{:S(2)}) copy-start(f32[48,3072]{1,0:T(8,128)} %get-tuple-element.95) | copy-start | bytes 1769476
  244.8 3.5 %copy-start.5 = (f32[192,768]{1,0:T(8,128)S(1)}, f32[192,768]{1,0:T(8,128)}, u32[]{:S(2)}) copy-start(f32[192,768]{1,0:T(8,128)} %get-tuple-element.96) | copy-start | bytes 1769476
where the time goes:
time: 250 us; the launch traced here: 249 us
  Pallas kernels  224 us (90%)
  local copies, waits for them, and re-layouts  13.9 us (6%)
  waiting for transfers between devices  4.09 us (2%)
  other arithmetic  3.93 us (2%)
  starting transfers between devices  2.79 us (1%)
    pallas_call x1, Pallas kernels, reduce_all(): pl.pallas_call(functools.partial(reduce_kernel, planes), out_shape=[sds((...  79.7 us
    pallas_call x1, Pallas kernels, forward_attention(): pl.pallas_call(functools.partial(forward_kernel, planes), out_shape=[sds(...  67.6 us
    pallas_call x1, Pallas kernels, dense_layers(): pl.pallas_call(functools.partial(dense_kernel, planes), out_shape=[sds((p...  47.1 us
    pallas_call x1, Pallas kernels, attend_back(): pl.pallas_call(backward_kernel, out_shape=[jax.ShapeDtypeStruct((count, W...  29.2 us
    unnamed x33, local copies, waits for them, and re-layouts  8.2 us
  transfers between devices with their start and end apart: 3, of which 1 were waited for; matrix products, arithmetic and copies ran while one was open for 0% of the time, Pallas kernels for 12%

commit v1 on v0

--- a/solution.py
+++ b/solution.py
@@ -90,7 +90,7 @@
         dk = jnp.dot(grad_scores, qexp, preferred_element_type=jnp.float32)
         dv = jnp.dot(probs.astype(jnp.bfloat16), doexp, preferred_element_type=jnp.float32)
         dq = tn(grad_scores, keys)
-        dq_ref[pl.ds(q_rows, BLK), :] = (fold_heads(dq, 0) * DH ** (-0.5)).astype(jnp.bfloat16)
+        dq_ref[pl.ds(q_rows, BLK), :] = fold_heads(dq, 0).astype(jnp.bfloat16)
         for s in range(SLOTS):
             k_s, v_s = dk[s * BLK : (s + 1) * BLK], dv[s * BLK : (s + 1) * BLK]
             at = pl.ds(rows[s], BLK)
@@ -144,7 +144,6 @@
 
 
 CHUNK_ORDER = (0, 1, 2, 4, 3, 5, 6, 7)
-JORDER = (3, 1, 2, 0)
 
 
 def slot_tables(plane, y_at, core, x_at, at, lengths, order, rand_own, rand_got, idx_ref, live_ref):
@@ -217,11 +216,17 @@
     return fold_heads(tn(probs, values), 64).astype(jnp.bfloat16)
 
 
-def forward_kernel(planes, tok_ref, wq_ref, wkv_ref, len_ref, ord_ref, rand_vm, rand_sm, *refs):
-    kv_out, q_ref, x_out, ctx_out, lse_ref, idx_ref, live_ref = refs[:7]
-    xs, kv, ctx, rand_got, rand_two = refs[7:12]
-    x_send, x_recv, k_send, k_recv, up_send, up_recv, dn_send, dn_recv = refs[12:20]
-    f_send, f_recv, g_send, g_recv, s_sem, o_send, o_recv, r_send, r_recv, l_sem = refs[20:30]
+def forward_kernel(planes, tok_ref, wq_in, wk_in, wv_in, len_ref, ord_ref, rand_vm, rand_sm, *refs):
+    kv_out, q_ref, x_out, ctx_out, lse_ref, idx_ref, live_ref, wq_out, wkv_out = refs[:9]
+    xs, kv, ctx, rand_got, rand_two, w_full, wq_ref, wkv_ref = refs[9:17]
+    x_send, x_recv, k_send, k_recv, up_send, up_recv, dn_send, dn_recv = refs[17:25]
+    f_send, f_recv, g_send, g_recv, s_sem, o_send, o_recv, r_send, r_recv, l_sem = refs[25:35]
+    weights = [
+        pltpu.make_async_copy(w, w_full.at[n], l_sem.at[2 + n])
+        for n, w in enumerate((wk_in, wv_in, wq_in))
+    ]
+    for copy in weights:
+        copy.start()
     plane, y_at, core, x_at = place()
     piece = tok_ref.shape[0]
     rows = piece // 2
@@ -254,6 +259,25 @@
     rand_trade.start()
     for c in (2, 4, 3, 5):
         hops[c].start()
+
+    wq_ref[:, WQ:] = jnp.zeros((wq_ref.shape[0], WIN - WQ), jnp.bfloat16)
+    for copy in weights:
+        copy.wait()
+    for g in range(4):
+
+        @pl.when(y_at * 2 + x_at == g)
+        def _(g=g):
+            cols = slice(g * WQ, (g + 1) * WQ)
+            wkv_ref[:, :WQ] = w_full[0, :, cols]
+            wkv_ref[:, WQ:] = w_full[1, :, cols]
+            wq_ref[:, :WQ] = w_full[2, :, cols] * jnp.bfloat16(DH ** (-0.5))
+
+    hand_on = [
+        pltpu.make_async_copy(wq_ref, wq_out, l_sem.at[5]),
+        pltpu.make_async_copy(wkv_ref, wkv_out, l_sem.at[6]),
+    ]
+    for copy in hand_on:
+        copy.start()
 
     def kv_rows(part_at, c):
         return kv.at[pl.ds((part_at * part + c * rows) // BLK, rows // BLK)]
@@ -285,24 +309,6 @@
             pass_down[c].start()
 
     for n, c in enumerate(CHUNK_ORDER):
-        if n == 2:
-            rand_trade.wait()
-            to_scalar = pltpu.make_async_copy(rand_got, rand_two, l_sem.at[0])
-            to_scalar.start()
-            to_scalar.wait()
-            slot_tables(
-                plane,
-                y_at,
-                core,
-                x_at,
-                dict(piece_blocks=piece // BLK, seqs=len_ref.shape[0]),
-                len_ref,
-                ord_ref,
-                rand_sm,
-                rand_two,
-                idx_ref,
-                live_ref,
-            )
         if c >= 2:
             hops[c].wait_recv()
         if c == 2:
@@ -328,7 +334,25 @@
         ).astype(jnp.bfloat16)
         if n >= 3:
             relay(CHUNK_ORDER[n - 3])
-    for c in CHUNK_ORDER[5:]:
+    relay(CHUNK_ORDER[5])
+    rand_trade.wait()
+    to_scalar = pltpu.make_async_copy(rand_got, rand_two, l_sem.at[0])
+    to_scalar.start()
+    to_scalar.wait()
+    slot_tables(
+        plane,
+        y_at,
+        core,
+        x_at,
+        dict(piece_blocks=piece // BLK, seqs=len_ref.shape[0]),
+        len_ref,
+        ord_ref,
+        rand_sm,
+        rand_two,
+        idx_ref,
+        live_ref,
+    )
+    for c in CHUNK_ORDER[6:]:
         relay(c)
     for c in range(8):
         to_core[c].wait_recv()
@@ -344,29 +368,45 @@
     saved = pltpu.make_async_copy(kv, kv_out, l_sem.at[1])
     saved.start()
     per = piece // BLK
-    trades = {}
-    for j in JORDER:
-
-        def step(n, carry, j=j):
-            done = attend_block(j * per + n, idx_ref, live_ref, q_ref, kv, lse_ref)
+
+    def part_of(turn):
+        middle = turn - 2
+        j = jnp.where(turn < 2, 3, jnp.where(turn < 6, 1 + lax.rem(turn, 2), 0))
+        half = jnp.where(turn < 2, turn, jnp.where(turn < 6, middle // 2, turn - 6))
+        return j, half
+
+    def trade(turn):
+        j, half = part_of(turn)
+        span = pl.ds(pl.multiple_of(half * rows, rows), rows)
+        return remote(
+            ctx.at[j, span],
+            ctx_out.at[span, pl.ds(pl.multiple_of(j * WIN, WIN), WIN)],
+            o_send,
+            o_recv,
+            turn,
+            device_at(plane, y_at ^ (j >> 1), core, x_at ^ (j & 1)),
+        )
+
+    def attend_part(turn, carry):
+        j, half = part_of(turn)
+
+        def step(n, carry):
             at = pl.ds(pl.multiple_of(n * BLK, BLK), BLK)
-            if j:
-                ctx[j - 1, at, :] = done
-            else:
-                ctx_out[at, 0:WIN] = done
+            ctx[j, at, :] = attend_block(j * per + n, idx_ref, live_ref, q_ref, kv, lse_ref)
             return carry
 
-        lax.fori_loop(0, per, step, 0, unroll=2)
-        if j:
-            trades[j] = remote(
-                ctx.at[j - 1],
-                ctx_out.at[:, pl.ds(j * WIN, WIN)],
-                o_send,
-                o_recv,
-                j - 1,
-                device_at(plane, y_at ^ (j >> 1), core, x_at ^ (j & 1)),
-            )
-            trades[j].start()
+        first = half * (per // 2)
+        for n in range(per // 2):
+            step(first + n, 0)
+
+        @pl.when(turn < 6)
+        def _():
+            trade(turn).start()
+
+        return carry
+
+    lax.fori_loop(0, 8, attend_part, 0)
+    ctx_out[:, 0:WIN] = ctx[0]
     for c in (2, 4, 3, 5, 6, 7):
         hops[c].wait_send()
     for c in range(8):
@@ -384,11 +424,17 @@
             pass_up[c].wait_send()
 
     saved.wait()
-    for j in (3, 1, 2):
-        trades[j].wait()
-
-
-def forward_attention(tokens, wq_own, wkv_own, lengths, seq_order, rand_row, planes):
+    for copy in hand_on:
+        copy.wait()
+
+    def settle(turn, carry):
+        trade(turn).wait()
+        return carry
+
+    lax.fori_loop(0, 6, settle, 0)
+
+
+def forward_attention(tokens, w_query, w_key, w_value, lengths, seq_order, rand_row, planes):
     piece, width = tokens.shape
     dma, low = pltpu.SemaphoreType.DMA, jnp.bfloat16
     sds = jax.ShapeDtypeStruct
@@ -403,22 +449,27 @@
             sds((blocks, WQ), jnp.float32),
             sds((blocks * SLOTS,), jnp.int32),
             sds((blocks * SLOTS,), jnp.int32),
+            sds((width, WIN), low),
+            sds((width, 2 * WQ), low),
         ],
-        in_specs=[VMEM] * 3 + [SMEM] * 2 + [VMEM, SMEM],
-        out_specs=[ANY, VMEM, ANY, VMEM, VMEM, SMEM, SMEM],
+        in_specs=[VMEM] + [ANY] * 3 + [SMEM] * 2 + [VMEM, SMEM],
+        out_specs=[ANY, VMEM, ANY, VMEM, VMEM, SMEM, SMEM, ANY, ANY],
         scratch_shapes=[
             pltpu.VMEM((3 * piece, width), low),
             pltpu.VMEM((24 * piece // BLK, BLK, 2 * WQ), low),
-            pltpu.VMEM((3, piece, WIN), low),
+            pltpu.VMEM((4, piece, WIN), low),
             pltpu.VMEM(rand_row.shape, jnp.int32),
             pltpu.SMEM(rand_row.shape, jnp.int32),
+            pltpu.VMEM((3, width, width), low),
+            pltpu.VMEM((width, WIN), low),
+            pltpu.VMEM((width, 2 * WQ), low),
             dma((6,)),
             dma((6,)),
         ]
         + [dma((8,))] * 11
-        + [dma((3,))] * 2
+        + [dma((6,))] * 2
         + [dma((1,))] * 2
-        + [dma((2,))],
+        + [dma((7,))],
         compiler_params=pltpu.CompilerParams(
             collective_id=0, has_side_effects=True, vmem_limit_bytes=62 << 20
         ),
@@ -426,7 +477,7 @@
             flops=2 * 4 * piece * width * 640, bytes_accessed=40 << 20, transcendentals=0
         ),
         name="forward_attention",
-    )(tokens, wq_own, wkv_own, lengths, seq_order, rand_row, rand_row)
+    )(tokens, w_query, w_key, w_value, lengths, seq_order, rand_row, rand_row)
 
 
 def attend_back(idx, live, queries, grads, level, keys_values):
@@ -463,7 +514,7 @@
     line_out, line_in = refs[54:57], refs[57:60]
     l_sem, i_sem, c_s, c_r, u_s, u_r, d_s, d_r, x_s, x_r = refs[60:70]
     pk_s, pk_r, pz_s, pz_r, pf_s, pf_r = refs[70:76]
-    w2_s, w2_r, w3_s, w3_r, w4_s, w4_r = refs[76:82]
+    w2_s, w2_r, w3_s, w3_r, w4_s, w4_r, w1_s, w1_r = refs[76:84]
     plane, y_at, core, x_at = place()
     piece = tok_out.shape[0]
     part = 4 * piece
@@ -532,11 +583,13 @@
 
     lax.fori_loop(0, 4, begin_mid, 0)
     inputs = [(pair_in[2 * n], keep[n]) for n in range(3)]
-    inputs += [(pair_in[2 * n + 1], give[n]) for n in range(3)]
+    inputs += [(pair_in[2 * n + 1], give[n]) for n in (0, 2)]
     inputs += [(wq_in, wq), (wkv_in, wkv), (dq_in, dq), (x_in, xs), (one_in, one)]
     inputs = [pltpu.make_async_copy(src, dst, i_sem.at[n]) for n, (src, dst) in enumerate(inputs)]
     for copy in inputs:
         copy.start()
+    w1 = remote(pair_in[3], give[1], w1_s, w1_r, 0, by_y)
+    w1.start()
 
     def both(turn, r, j):
         to_core(turn, r, j).wait_recv()
@@ -562,11 +615,13 @@
 
     lax.fori_loop(0, 4, spread, 0)
 
-    for copy in inputs[:6]:
+    for copy in inputs[:5]:
         copy.wait()
     halves = [keep[0].shape[2] // 2, keep[1].shape[2] // 2]
-    w2 = []
-    for n in range(3):
+    w2 = {}
+    for n in (0, 2, 1):
+        if n == 1:
+            w1.wait()
 
         def merge(p, carry, n=n):
             keep[n][p] = (keep[n][p].astype(f32) + give[n][p].astype(f32)).astype(low)
@@ -575,11 +630,11 @@
         lax.fori_loop(0, planes, merge, 0)
         if n < 2:
             cols = pl.ds(pl.multiple_of((1 - x_at) * halves[n], 128), halves[n])
-            w2.append(remote(keep[n].at[:, :, cols], got[n], w2_s, w2_r, n, by_x))
+            w2[n] = remote(keep[n].at[:, :, cols], got[n], w2_s, w2_r, n, by_x)
         else:
-            w2.append(remote(keep[n].at[:, 1 - y_at], got[n], w2_s, w2_r, n, by_y))
+            w2[n] = remote(keep[n].at[:, 1 - y_at], got[n], w2_s, w2_r, n, by_y)
         w2[n].start()
-    for copy in inputs[6:]:
+    for copy in inputs[5:]:
         copy.wait()
     acc[...] = jnp.zeros_like(acc)
 
@@ -669,6 +724,7 @@
     outer(0)
 
     share = p_slab.shape[3]
+    acc[:, 2 * WQ :] *= DH ** (-0.5)
     for p in range(planes):
         for y in range(2):
             for k in range(2):
@@ -755,7 +811,7 @@
         side_out[:, side * width : (side + 1) * width] = done[:share]
         norm_out[:, side * width : (side + 1) * width] = done[share : share + 8]
 
-    for copy in w2 + pz + [pk]:
+    for copy in list(w2.values()) + pz + [pk]:
         copy.wait_send()
 
     def settle(n, carry):
@@ -848,7 +904,8 @@
         + [dma((3,))] * 2
         + [dma((3,))] * 2
         + [dma((6 * rest,))] * 2
-        + [dma((3,))] * 2,
+        + [dma((3,))] * 2
+        + [dma((1,))] * 2,
         compiler_params=pltpu.CompilerParams(
             collective_id=1, has_side_effects=True, vmem_limit_bytes=60 << 20
         ),
@@ -868,7 +925,7 @@
     b1_ref,
     g2_ref,
     b2_ref,
-    wout_ref,
+    wout_in,
     wup_in,
     wdown_in,
     *refs,
@@ -877,6 +934,7 @@
     wup, wdown, acc, x1, s1, g_two, nl, hid, slope, gp, gm, ga = refs[9:21]
     dctx, up_loc, out_loc, down_loc, up_got, out_got, down_got, down_sum = refs[21:29]
     w_sem, mv_sem, do_s, do_r, up_s, up_r, out_s, out_r, down_s, down_r = refs[29:39]
+    wout_ref = refs[39]
     plane, y_at, core, x_at = place()
     piece, width = tok_ref.shape
     share = up_loc.shape[2]
@@ -884,6 +942,16 @@
     pairs = 2 * planes
     group = y_at * 2 + x_at
     f32 = jnp.float32
+    fetch = [
+        pltpu.make_async_copy(
+            wout_in.at[pl.ds(pl.multiple_of((group ^ j) * WQ, WQ), WQ)],
+            wout_ref.at[pl.ds(j * WIN + WIN - WQ, WQ)],
+            w_sem.at[2 + j],
+        )
+        for j in range(4)
+    ]
+    for copy in fetch:
+        copy.start()
     bring = [
         pltpu.make_async_copy(wup_in, wup, w_sem.at[0]),
         pltpu.make_async_copy(wdown_in, wdown, w_sem.at[1]),
@@ -912,6 +980,10 @@
     def fold(v):
         return v[:8] + v[8:16] + v[16:24] + v[24:]
 
+    for j in range(4):
+        wout_ref[j * WIN : j * WIN + WIN - WQ, :] = jnp.zeros((WIN - WQ, width), jnp.bfloat16)
+    for copy in fetch:
+        copy.wait()
     acc[...] = jnp.dot(ctx_ref[...], wout_ref[...], preferred_element_type=f32)
     g1, b1, g2, b2 = (r[...].reshape(1, width) for r in (g1_ref, b1_ref, g2_ref, b2_ref))
 
@@ -1009,34 +1081,41 @@
         else:
             do_out[pl.ds(0, piece), :] = part
 
-    to_core = []
     tile = 2 * WQ
     per = tile // (2 * slab)
-    for t in range(hid.shape[1] // tile):
-        cell = tn(hid[:, t * tile : (t + 1) * tile], gm[...])
+    tiles = wide // tile
+
+    def down_copy(t):
+        span = pl.ds(t * per, per)
+        return remote(down_loc.at[1 - core, span], down_got.at[span], down_s, down_r, t, by_core)
+
+    def up_copy(t):
+        span = cols_of(t)
+        return remote(
+            up_loc.at[1 - core, :, :, span], up_got.at[:, :, span], up_s, up_r, t, by_core
+        )
+
+    def make_down(t, carry):
+        cell = tn(hid[:, cols_of(t)], gm[...])
         for n in range(per):
             for k in range(2):
                 at = (n * 2 + k) * slab
                 down_loc[k, t * per + n] = cell[at : at + slab].astype(low)
-        span = pl.ds(t * per, per)
-        to_core.append(
-            remote(down_loc.at[1 - core, span], down_got.at[span], down_s, down_r, t, by_core)
-        )
-        to_core[-1].start()
-    ups = []
-    for t in range(gp.shape[1] // tile):
-        span = pl.ds(t * tile, tile)
-        cell = tn(nl[...], gp[:, t * tile : (t + 1) * tile])
+        down_copy(t).start()
+        return carry
+
+    lax.fori_loop(0, tiles, make_down, 0)
+
+    def make_up(t, carry):
+        cell = tn(nl[...], gp[:, cols_of(t)])
         for q in range(pairs):
             for k in range(2):
                 at = (q * 2 + k) * share
-                up_loc[k, q, :, t * tile : (t + 1) * tile] = cell[at : at + share].astype(low)
-        ups.append(
-            remote(
-                up_loc.at[1 - core, :, :, span], up_got.at[:, :, span], up_s, up_r, t, by_core
-            )
-        )
-        ups[-1].start()
+                up_loc[k, q, :, cols_of(t)] = cell[at : at + share].astype(low)
+        up_copy(t).start()
+        return carry
+
+    lax.fori_loop(0, tiles, make_up, 0)
     per_group = pairs // 4
     for j in range(4):
         cell = tn(ctx_ref[:, j * WIN : (j + 1) * WIN], ga[...])
@@ -1057,22 +1136,29 @@
         moved[-1].start()
 
     half = width // 2
-    for n, copy in enumerate(to_core):
-        copy.wait_recv()
-        for q in range(n * per, (n + 1) * per):
+
+    def sum_down(t, carry):
+        down_copy(t).wait_recv()
+        for n in range(per):
+            q = t * per + n
             total = (
                 down_loc[core, q].astype(jnp.float32) + down_got[q].astype(jnp.float32)
             ).astype(low)
             down_sum[0, q] = total[:, :half]
             down_sum[1, q] = total[:, half:]
+        return carry
+
+    lax.fori_loop(0, tiles, sum_down, 0)
     move(down_sum.at[x_at], down_keep)
     move(down_sum.at[1 - x_at], down_give)
-    for copy in ups:
-        copy.wait_recv()
-    for p in range(planes):
-        for y in range(2):
-            q = p * 2 + y
-            up_got[q] = (up_loc[core, q].astype(jnp.float32) + up_got[q].astype(jnp.float32)).astype(low)
+
+    def sum_up(q, carry):
+        up_got[q] = (up_loc[core, q].astype(jnp.float32) + up_got[q].astype(jnp.float32)).astype(low)
+        return carry
+
+    for t in range(tiles):
+        up_copy(t).wait_recv()
+    lax.fori_loop(0, pairs, sum_up, 0)
     outs.wait_recv()
     for p in range(planes):
         for y in range(2):
@@ -1085,8 +1171,10 @@
             move(got.at[p * 2 + 1 - y_at], give.at[p])
     for copy in trades:
         copy.wait()
-    for copy in to_core + ups + [outs]:
-        copy.wait_send()
+    for t in range(tiles):
+        down_copy(t).wait_send()
+        up_copy(t).wait_send()
+    outs.wait_send()
     for copy in moved:
         copy.wait()
 
@@ -1108,7 +1196,7 @@
         + [sds(up, low)] * 2
         + [sds(out, low)] * 2
         + [sds(down, low)] * 2,
-        in_specs=[VMEM] * 8 + [ANY] * 2,
+        in_specs=[VMEM] * 7 + [ANY] * 3,
         out_specs=[VMEM] * 3 + [ANY] * 6,
         scratch_shapes=[
             vm(w_up.shape, low),
@@ -1131,13 +1219,14 @@
             vm((pairs, share + tall, width), low),
             vm((pairs, slab, width), low),
             vm((2, pairs, slab, width // 2), low),
-            dma((2,)),
+            dma((6,)),
             dma((2 + 4 * planes,)),
         ]
         + [dma((3,))] * 2
         + [dma((tiles,))] * 2
         + [dma((1,))] * 2
-        + [dma((tiles,))] * 2,
+        + [dma((tiles,))] * 2
+        + [vm((4 * WIN, width), low)],
         compiler_params=pltpu.CompilerParams(
             collective_id=2, has_side_effects=True, vmem_limit_bytes=62 << 20
         ),
@@ -1148,8 +1237,32 @@
     )(tokens, ctx, cotangent, *norms, wout, w_up, w_down)
 
 
-def pick(array, at, axis):
-    return lax.dynamic_index_in_dim(array, at, axis, keepdims=False)
+def finish_kernel(share, *refs):
+    count = (len(refs) - 5) // 2
+    for n in range(count):
+        refs[count + 1 + n][...] = refs[n][...]
+    seq_at = lax.axis_index("seq")
+    rows = refs[count][...]
+    width = rows.shape[1]
+    spot = lax.broadcasted_iota(jnp.int32, (width, 128), 0) - seq_at * share
+    chosen = (spot == lax.broadcasted_iota(jnp.int32, (width, 128), 1)).astype(jnp.float32)
+    picked = jnp.dot(
+        rows, chosen, preferred_element_type=jnp.float32, precision=lax.Precision.HIGHEST
+    )
+    for n in range(4):
+        refs[2 * count + 1 + n][...] = picked[n, :share]
+
+
+def finish(arrays, norm_rows, share):
+    sds = jax.ShapeDtypeStruct
+    return pl.pallas_call(
+        functools.partial(finish_kernel, share),
+        out_shape=[sds(v.shape, v.dtype) for v in arrays] + [sds((share,), jnp.float32)] * 4,
+        in_specs=[VMEM] * (len(arrays) + 1),
+        out_specs=[VMEM] * (len(arrays) + 4),
+        compiler_params=pltpu.CompilerParams(vmem_limit_bytes=62 << 20),
+        name="finish",
+    )(*arrays, norm_rows)
 
 
 def body(
@@ -1177,44 +1290,31 @@
     plane, y_at, core = seq_at // 4, (seq_at // 2) % 2, seq_at % 2
     group = y_at * 2 + x_at
 
-    def columns(weights):
-        return lax.dynamic_slice_in_dim(weights, group * WQ, WQ, 1)
-
-    wq_own = jnp.pad(columns(w_query) * jnp.bfloat16(DH ** (-0.5)), ((0, 0), (0, WIN - WQ)))
-    wkv_own = jnp.concatenate([columns(w_key), columns(w_value)], axis=1)
-    order = [group ^ j for j in range(4)]
-    wout_own = jnp.concatenate(
-        [
-            jnp.pad(lax.dynamic_slice_in_dim(w_out, g * WQ, WQ, 0), ((WIN - WQ, 0), (0, 0)))
-            for g in order
-        ],
-        axis=0,
-    )
-
     flat = rand_blocks.reshape(1, -1)
     rand_row = jnp.pad(flat, ((0, 0), (0, 128 - flat.shape[1])))
-    keys_values, queries, stretch, context_tok, level, idx, live = forward_attention(
-        tokens, wq_own, wkv_own, lengths, seq_order, rand_row, planes
+    keys_values, queries, stretch, context_tok, level, idx, live, wq_own, wkv_own = (
+        forward_attention(
+            tokens, w_query, w_key, w_value, lengths, seq_order, rand_row, planes
+        )
     )
     share = width // seqs
     norms = [gain_attn, shift_attn, gain_mlp, shift_mlp]
     output, grad_one, grad_ctx, up_keep, up_give, out_keep, out_give, down_keep, down_give = (
-        dense_layers(tokens, context_tok, cotangent, norms, wout_own, w_up, w_down, planes)
+        dense_layers(tokens, context_tok, cotangent, norms, w_out, w_up, w_down, planes)
     )
     up_pair = (up_keep, xor_swap(up_give, 4))
-    out_pair = (out_keep, xor_swap(out_give, 4))
+    out_pair = (out_keep, out_give)
     two_y = (planes, 2) + down_keep.shape[1:]
     down_pair = (down_keep.reshape(two_y), xor_swap(down_give, 1).reshape(two_y))
 
     grad_q, grad_kv = attend_back(
         idx, live, queries, grad_ctx, level, keys_values.reshape(-1, 2 * WQ)
     )
-    wq_plain = jnp.pad(columns(w_query), ((0, 0), (0, WIN - WQ)))
     grad_tokens, grad_wq, grad_wk, grad_wv, up_total, out_total, norm_rows, down_total = reduce_all(
         grad_kv,
         grad_q,
         stretch,
-        wq_plain,
+        wq_own,
         wkv_own,
         grad_one,
         up_pair,
@@ -1223,22 +1323,25 @@
         planes,
     )
 
-    def norm_grad(n):
-        return lax.dynamic_slice_in_dim(norm_rows[n], seq_at * share, share, 0)
-
+    finals = finish(
+        (grad_tokens, grad_wq, grad_wk, grad_wv, out_total, up_total, down_total), norm_rows, share
+    )
+
+    grad_tokens, grad_wq, grad_wk, grad_wv, grad_out, grad_up, grad_down = finals[:7]
+    gain_one, shift_one, gain_two, shift_two = finals[7:]
     return (
         output,
         grad_tokens,
         grad_wq,
         grad_wk,
         grad_wv,
-        out_total,
-        norm_grad(0),
-        norm_grad(1),
-        up_total,
-        down_total,
-        norm_grad(2),
-        norm_grad(3),
+        grad_out,
+        gain_one,
+        shift_one,
+        grad_up,
+        grad_down,
+        gain_two,
+        shift_two,
     )
 
 

time: 250 us -> 230 us (0.920)
  local copies, waits for them, and re-layouts: 13.9 us -> 3.63 us
  waiting for transfers between devices: 4.09 us -> 0.01 us
  other arithmetic: 3.93 us -> 0 us
    unnamed x33 -> x8, local copies, waits for them, and re-layouts: 8.2 us -> 3.02 us
    pallas_call x1, Pallas kernels: 67.6 us -> 62.5 us  [forward_attention(): pl.pallas_call(functools.partial(forward_kernel, planes), out_shape=[sds(...]
    ppermute x3 -> x2, waiting for transfers between devices: 4.09 us -> 0.01 us  [xor_swap(): return lax.ppermute(value, AXES, [(d, d ^ bits) for d in range(count)])]
    pallas_call x0 -> x1, Pallas kernels: none -> 3.93 us  [finish(): pl.pallas_call(functools.partial(finish_kernel, share), out_shape=[sds(v....]
    dynamic_slice x6 -> x0, local copies, waits for them, and re-layouts: 2.58 us -> none  [the longest x4 2.33 us: norm_grad(): return lax.dynamic_slice_in_dim(norm_rows[n], seq_at * share, share, 0)]
  transfers between devices with their start and end apart: 3 -> 2, of which waited for: 1 -> 0; matrix products, arithmetic and copies ran while one was open for 0% -> 0% of each run, Pallas kernels for 12% -> 13%
where the time goes in v1:
time: 230 us; the launch traced here: 229 us
  Pallas kernels  223 us (97%)
  local copies, waits for them, and re-layouts  3.63 us (2%)
    pallas_call x1, Pallas kernels, reduce_all(): pl.pallas_call(functools.partial(reduce_kernel, planes), out_shape=[sds((...  80.1 us
    pallas_call x1, Pallas kernels, forward_attention(): pl.pallas_call(functools.partial(forward_kernel, planes), out_shape=[sds(...  62.5 us
    pallas_call x1, Pallas kernels, dense_layers(): pl.pallas_call(functools.partial(dense_kernel, planes), out_shape=[sds((p...  47.2 us
    pallas_call x1, Pallas kernels, attend_back(): pl.pallas_call(backward_kernel, out_shape=[jax.ShapeDtypeStruct((count, W...  29.1 us
  transfers between devices with their start and end apart: 2, of which 0 were waited for; matrix products, arithmetic and copies ran while one was open for 0% of the time, Pallas kernels for 13%

profile of v1, /device:TPU:24, one launch (start us, length us, event | category | flops | bytes accessed | tf_op | source)
XLA Modules:
  0.0 229.3 jit_solution(15081964279630002183)
XLA Ops:
  0.6 0.8 copy.28
  1.4 0.1 reshape.36
  1.5 0.5 pad.4.rand_vm.rand_sm
  2.0 62.5 %forward_attention.1 = (bf16[192,64,384]{2,1,0:T(8,128)(2,1)}, bf16[2048,256]{1,0:T(8,128)(2,1)}, bf16[2048,768]{1,0:T(8,128)(2,1)}, bf16[512,1024]{1,0:T(8,128)...) custom-call(bf16[512,768]{1,0:T(8,128)(2,1)} %tok_ref.3, ...), custom_call_target="tpu_custom_call" | custom-call | flops 2013265920 | bytes 41943040 | tf_op jit(solution)/shard_map/forward_attention/pallas_call | solution.py:442
  64.5 47.2 %dense_layers.1 = (bf16[512,768]{1,0:T(8,128)(2,1)}, f32[512,768]{1,0:T(8,128)}, bf16[2048,256]{1,0:T(8,128)(2,1)}, bf16[4,48,3072]{2,1,0:T(8,128)(2,1)}, bf16[4...) custom-call(bf16[512,768]{1,0:T(8,128)(2,1)} %tok_ref.3, ...), custom_call_target="tpu_custom_call" | custom-call | flops 16911433728 | bytes 31457280 | tf_op jit(solution)/shard_map/dense_layers/pallas_call | solution.py:1193
  111.8 0.7 collective-permute-start
  112.5 1.4 collective-permute-start.1
  113.9 29.1 %attend_back.1 = (bf16[2048,256]{1,0:T(8,128)(2,1)}, bf16[12288,384]{1,0:T(8,128)(2,1)}) custom-call(s32[256]{0:T(256)} %get-tuple-element.53.idx_ref, s32[256]{0:T(256)} %get-tuple-element.54.live_ref, bf16[2048,256]{1,0:T(8,128)(2,1)} %get-tuple-element.55.q_ref, bf16[2048,256]{1,0:T(8,128)(2,1)} %get-tuple-element.56.do_ref, ...), custom_call_target="tpu_custom_call" | custom-call | flops 16106127360 | bytes 18874368 | tf_op jit(solution)/shard_map/attend_back/pallas_call | solution.py:487
  143.0 0.0 collective-permute-done.refs_7_
  143.0 0.0 copy-start
  143.0 0.0 collective-permute-done.1
  143.0 0.0 copy-start.1
  143.1 1.0 copy-done
  144.0 0.4 copy-done.1
  144.4 80.1 %reduce_all.1 = (f32[512,768]{1,0:T(8,128)}, f32[48,768]{1,0:T(8,128)}, f32[48,768]{1,0:T(8,128)}, f32[48,768]{1,0:T(8,128)}, f32[48,3072]{1,0:T(8,128)}, /*inde...) custom-call(bf16[12288,384]{1,0:T(8,128)(2,1)} %get-tuple-element.59.refs_0_, ...), custom_call_target="tpu_custom_call" | custom-call | flops 4026531840 | bytes 41943040 | tf_op jit(solution)/shard_map/reduce_all/pallas_call | solution.py:861
  224.5 0.0 copy-start.2
  224.5 3.9 %finish.1 = (f32[512,768]{1,0:T(8,128)}, f32[48,768]{1,0:T(8,128)}, f32[48,768]{1,0:T(8,128)}, f32[48,768]{1,0:T(8,128)}, f32[48,768]{1,0:T(8,128)}, /*index=5*/...) custom-call(f32[512,768]{1,0:T(8,128)} %get-tuple-element.71.refs_0_, ...), custom_call_target="tpu_custom_call" | custom-call | tf_op jit(solution)/shard_map/finish/pallas_call | solution.py:1258
  228.4 0.0 copy-done.2
  228.4 0.9 copy.30
Async XLA Ops:
  111.8 31.2 %collective-permute-start = (bf16[4,48,3072]{2,1,0:T(8,128)(2,1)}, bf16[4,48,3072]{2,1,0:T(8,128)(2,1)S(1)}, u32[]{:S(2)}, u32[]{:S(2)}) collective-permute-start(bf16[4,48,3072]{2,1,0:T(8,128)(2,1)} %get-tuple-element.66), channel_id=1, source_target_pairs={{0,4},{1,5},{2,6},{3,7},{4,0},{5,1},{6,2},{7,3},{8,12},{9,13},{10,... | collective-permute-start | bytes 3538952 | tf_op jit(solution)/shard_map/ppermute | solution.py:25
  112.5 30.5 %collective-permute-start.1 = (bf16[8,192,384]{2,1,0:T(8,128)(2,1)}, bf16[8,192,384]{2,1,0:T(8,128)(2,1)S(1)}, u32[]{:S(2)}, u32[]{:S(2)}) collective-permute-start(bf16[8,192,384]{2,1,0:T(8,128)(2,1)} %get-tuple-element.70), channel_id=1, source_target_pairs={{0,1},{1,0},{2,3},{3,2},{4,5},{5,4},{6,7},{7,6},{8,9},{9,8},{10,11... | collective-permute-start | bytes 3538952 | tf_op jit(solution)/shard_map/ppermute | solution.py:25
  143.0 1.0 copy-start
  143.0 1.4 copy-start.1
  224.5 3.9 %copy-start.2 = (bf16[512,768]{1,0:T(8,128)(2,1)S(1)}, bf16[512,768]{1,0:T(8,128)(2,1)}, u32[]{:S(2)}) copy-start(bf16[512,768]{1,0:T(8,128)(2,1)} %get-tuple-element.102) | copy-start | bytes 2359300

commit v2 on v1

--- a/solution.py
+++ b/solution.py
@@ -51,7 +51,7 @@
     return lax.dot_general(a, b, (((0,), (0,)), ((), ())), preferred_element_type=jnp.float32)
 
 
-def backward_kernel(idx_ref, live_ref, q_ref, do_ref, lse_ref, *refs):
+def backward_kernel(idx_ref, live_ref, q_ref, do_ref, o_ref, lse_ref, *refs):
     kv_ref, dq_ref, dkv_ref, kv, acc, sems = refs
 
     def clear(n, carry):
@@ -72,23 +72,29 @@
         ]
         keys = jnp.concatenate([kv[pl.ds(r, BLK), 0:WIN] for r in rows], axis=0)
         values = jnp.concatenate([kv[pl.ds(r, BLK), 128 : 128 + WIN] for r in rows], axis=0)
+        product = do_ref[pl.ds(q_rows, BLK), :].astype(jnp.float32) * o_ref[
+            pl.ds(q_rows, BLK), :
+        ].astype(jnp.float32)
+        high = product.astype(jnp.bfloat16)
+        ones = jnp.ones((8, WIN), jnp.bfloat16)
+        inner = nt(ones, spread_heads(high, 64)) + nt(
+            ones, spread_heads((product - high.astype(jnp.float32)).astype(jnp.bfloat16), 64)
+        )
+        inner = inner[0:1]
+        level = lse_ref[pl.ds(i, 1), :]
         raw = nt(keys, qexp)
-        level = lse_ref[pl.ds(i, 1), :]
-        probs = jnp.concatenate(
-            [
-                jnp.exp(
-                    raw[s * BLK : (s + 1) * BLK]
-                    - (level + jnp.where(live_ref[i * SLOTS + s] > 0, 0.0, -NEG))
-                )
-                for s in range(SLOTS)
-            ],
-            axis=0,
-        )
         grad_probs = nt(values, doexp)
-        inner = jnp.sum(probs * grad_probs, axis=0, keepdims=True)
-        grad_scores = (probs * (grad_probs - inner)).astype(jnp.bfloat16)
+        probs, grad_scores = [], []
+        for s in range(SLOTS):
+            at = slice(s * BLK, (s + 1) * BLK)
+            off = level + jnp.where(live_ref[i * SLOTS + s] > 0, 0.0, -NEG)
+            p = jnp.exp(raw[at] - off)
+            probs.append(p.astype(jnp.bfloat16))
+            grad_scores.append((p * (grad_probs[at] - inner)).astype(jnp.bfloat16))
+        probs = jnp.concatenate(probs, axis=0)
+        grad_scores = jnp.concatenate(grad_scores, axis=0)
         dk = jnp.dot(grad_scores, qexp, preferred_element_type=jnp.float32)
-        dv = jnp.dot(probs.astype(jnp.bfloat16), doexp, preferred_element_type=jnp.float32)
+        dv = jnp.dot(probs, doexp, preferred_element_type=jnp.float32)
         dq = tn(grad_scores, keys)
         dq_ref[pl.ds(q_rows, BLK), :] = fold_heads(dq, 0).astype(jnp.bfloat16)
         for s in range(SLOTS):
@@ -192,7 +198,7 @@
             live_ref[i * SLOTS + s] = alive
         return carry
 
-    lax.fori_loop(0, 4 * per, one, 0)
+    lax.fori_loop(at["begin"], at["end"], one, 0)
 
 
 def attend_block(i, idx_ref, live_ref, q_ref, kv, lse_ref):
@@ -217,10 +223,10 @@
 
 
 def forward_kernel(planes, tok_ref, wq_in, wk_in, wv_in, len_ref, ord_ref, rand_vm, rand_sm, *refs):
-    kv_out, q_ref, x_out, ctx_out, lse_ref, idx_ref, live_ref, wq_out, wkv_out = refs[:9]
-    xs, kv, ctx, rand_got, rand_two, w_full, wq_ref, wkv_ref = refs[9:17]
-    x_send, x_recv, k_send, k_recv, up_send, up_recv, dn_send, dn_recv = refs[17:25]
-    f_send, f_recv, g_send, g_recv, s_sem, o_send, o_recv, r_send, r_recv, l_sem = refs[25:35]
+    kv_out, q_ref, x_out, ctx_out, lse_ref, idx_ref, live_ref, wq_out, wkv_out, ctx_keep = refs[:10]
+    xs, kv, ctx, rand_got, rand_two, w_full, wq_ref, wkv_ref = refs[10:18]
+    x_send, x_recv, k_send, k_recv, up_send, up_recv, dn_send, dn_recv = refs[18:26]
+    f_send, f_recv, g_send, g_recv, s_sem, o_send, o_recv, r_send, r_recv, l_sem = refs[26:36]
     weights = [
         pltpu.make_async_copy(w, w_full.at[n], l_sem.at[2 + n])
         for n, w in enumerate((wk_in, wv_in, wq_in))
@@ -308,7 +314,33 @@
             to_below[c].wait_recv()
             pass_down[c].start()
 
+    def tables(begin, end):
+        slot_tables(
+            plane,
+            y_at,
+            core,
+            x_at,
+            dict(piece_blocks=piece // BLK, seqs=len_ref.shape[0], begin=begin, end=end),
+            len_ref,
+            ord_ref,
+            rand_sm,
+            rand_two,
+            idx_ref,
+            live_ref,
+        )
+
+    query_blocks = part // BLK
     for n, c in enumerate(CHUNK_ORDER):
+        if n == 2:
+            rand_trade.wait()
+            to_scalar = pltpu.make_async_copy(rand_got, rand_two, l_sem.at[0])
+            to_scalar.start()
+            to_scalar.wait()
+            tables(0, query_blocks // 3)
+        if n == 4:
+            tables(query_blocks // 3, 2 * query_blocks // 3)
+        if n == 6:
+            tables(2 * query_blocks // 3, query_blocks)
         if c >= 2:
             hops[c].wait_recv()
         if c == 2:
@@ -334,25 +366,7 @@
         ).astype(jnp.bfloat16)
         if n >= 3:
             relay(CHUNK_ORDER[n - 3])
-    relay(CHUNK_ORDER[5])
-    rand_trade.wait()
-    to_scalar = pltpu.make_async_copy(rand_got, rand_two, l_sem.at[0])
-    to_scalar.start()
-    to_scalar.wait()
-    slot_tables(
-        plane,
-        y_at,
-        core,
-        x_at,
-        dict(piece_blocks=piece // BLK, seqs=len_ref.shape[0]),
-        len_ref,
-        ord_ref,
-        rand_sm,
-        rand_two,
-        idx_ref,
-        live_ref,
-    )
-    for c in CHUNK_ORDER[6:]:
+    for c in CHUNK_ORDER[5:]:
         relay(c)
     for c in range(8):
         to_core[c].wait_recv()
@@ -407,6 +421,8 @@
 
     lax.fori_loop(0, 8, attend_part, 0)
     ctx_out[:, 0:WIN] = ctx[0]
+    hand_on.append(pltpu.make_async_copy(ctx, ctx_keep, l_sem.at[7]))
+    hand_on[-1].start()
     for c in (2, 4, 3, 5, 6, 7):
         hops[c].wait_send()
     for c in range(8):
@@ -451,9 +467,10 @@
             sds((blocks * SLOTS,), jnp.int32),
             sds((width, WIN), low),
             sds((width, 2 * WQ), low),
+            sds((4, piece, WIN), low),
         ],
         in_specs=[VMEM] + [ANY] * 3 + [SMEM] * 2 + [VMEM, SMEM],
-        out_specs=[ANY, VMEM, ANY, VMEM, VMEM, SMEM, SMEM, ANY, ANY],
+        out_specs=[ANY, VMEM, ANY, VMEM, VMEM, SMEM, SMEM, ANY, ANY, ANY],
         scratch_shapes=[
             pltpu.VMEM((3 * piece, width), low),
             pltpu.VMEM((24 * piece // BLK, BLK, 2 * WQ), low),
@@ -469,7 +486,7 @@
         + [dma((8,))] * 11
         + [dma((6,))] * 2
         + [dma((1,))] * 2
-        + [dma((7,))],
+        + [dma((8,))],
         compiler_params=pltpu.CompilerParams(
             collective_id=0, has_side_effects=True, vmem_limit_bytes=62 << 20
         ),
@@ -480,14 +497,14 @@
     )(tokens, w_query, w_key, w_value, lengths, seq_order, rand_row, rand_row)
 
 
-def attend_back(idx, live, queries, grads, level, keys_values):
+def attend_back(idx, live, queries, grads, context, level, keys_values):
     rows, width = keys_values.shape[0] // 6, keys_values.shape[1]
     count = queries.shape[0]
     kv_shape = jax.ShapeDtypeStruct((6 * rows, width), jnp.bfloat16)
     return pl.pallas_call(
         backward_kernel,
         out_shape=[jax.ShapeDtypeStruct((count, WIN), jnp.bfloat16)] + [kv_shape],
-        in_specs=[SMEM, SMEM, VMEM, VMEM, VMEM, ANY],
+        in_specs=[SMEM, SMEM, VMEM, VMEM, VMEM, VMEM, ANY],
         out_specs=[VMEM] * 2,
         scratch_shapes=[
             pltpu.VMEM((6 * rows, width), jnp.bfloat16),
@@ -499,7 +516,7 @@
             flops=2 * 10 * count * 3 * 256 * 512, bytes_accessed=24 * rows * width, transcendentals=count * 3 * 512
         ),
         name="attend_back",
-    )(idx, live, queries, grads, level, keys_values)
+    )(idx, live, queries, grads, context, level, keys_values)
 
 
 def reduce_kernel(planes, *refs):
@@ -747,14 +764,35 @@
         )
         for g in range(1, planes)
     ]
+
+    def next_step(t, carry):
+        line_step(t)
+        return carry
+
+    lax.fori_loop(2, planes - 1, next_step, 0)
     for copy in pz:
         copy.start()
-
-    def next_step(t, carry):
-        line_step(t)
-        return carry
-
-    lax.fori_loop(2, planes - 1, next_step, 0)
+    w4 = []
+    for n in range(3):
+        fin[n][x_at] = two[n][plane]
+
+        @pl.when(has_below)
+        def _(n=n):
+            line_copy(n, 0, rest - 1).wait_recv()
+            fin[n][x_at] = (
+                fin[n][x_at].astype(f32) + line_in[n][0, rest - 1].astype(f32)
+            ).astype(low)
+
+        @pl.when(has_above)
+        def _(n=n):
+            line_copy(n, 1, rest - 1).wait_recv()
+            fin[n][x_at] = (
+                fin[n][x_at].astype(f32) + line_in[n][1, rest - 1].astype(f32)
+            ).astype(low)
+
+        w4.append(remote(fin[n].at[x_at], fin[n].at[x_at], w4_s, w4_r, n, by_x))
+        w4[n].start()
+
     for j in (3, 2, 1):
         to_owner(j).wait_recv()
         tok_out[...] += dx_in[j - 1].astype(f32)
@@ -771,27 +809,6 @@
     for copy in pf:
         copy.start()
     p_all[0] = p_fin[y_at]
-
-    w4 = []
-    for n in range(3):
-        fin[n][x_at] = two[n][plane]
-
-        @pl.when(has_below)
-        def _(n=n):
-            line_copy(n, 0, rest - 1).wait_recv()
-            fin[n][x_at] = (
-                fin[n][x_at].astype(f32) + line_in[n][0, rest - 1].astype(f32)
-            ).astype(low)
-
-        @pl.when(has_above)
-        def _(n=n):
-            line_copy(n, 1, rest - 1).wait_recv()
-            fin[n][x_at] = (
-                fin[n][x_at].astype(f32) + line_in[n][1, rest - 1].astype(f32)
-            ).astype(low)
-
-        w4.append(remote(fin[n].at[x_at], fin[n].at[x_at], w4_s, w4_r, n, by_x))
-        w4[n].start()
 
     for copy in pf:
         copy.wait()
@@ -963,8 +980,6 @@
         return device_at(plane, y_at ^ (j >> 1), core, x_at ^ (j & 1))
 
     by_core = device_at(plane, y_at, 1 - core, x_at)
-    greet([there(1), there(2), there(3), by_core])
-
     height, tile = 32, 2 * WQ
     wide = wup.shape[1]
 
@@ -998,7 +1013,7 @@
         nl[at, :] = (hat * g1 + b1).astype(jnp.bfloat16)
         return carry
 
-    lax.fori_loop(0, piece // height, norm_one, 0, unroll=2)
+    lax.fori_loop(0, piece // height, norm_one, 0, unroll=4)
     bring[0].wait()
 
     def expand(n, carry):
@@ -1014,7 +1029,7 @@
         )
         return carry
 
-    lax.fori_loop(0, wide // tile, expand, 0)
+    lax.fori_loop(0, wide // tile, expand, 0, unroll=2)
     bring[1].wait()
     acc[...] = jnp.dot(hid[...], wdown[...], preferred_element_type=f32)
     nothing = jnp.zeros((8, width), f32)
@@ -1035,7 +1050,7 @@
         gm[at, :] = grad.astype(jnp.bfloat16)
         return gain_sum, shift_sum
 
-    gain_two, shift_two = lax.fori_loop(0, piece // height, norm_two, (nothing, nothing), unroll=2)
+    gain_two, shift_two = lax.fori_loop(0, piece // height, norm_two, (nothing, nothing), unroll=4)
 
     def shrink(n, carry):
         at = cols_of(n)
@@ -1043,7 +1058,7 @@
         gp[:, at] = (back * slope[:, at]).astype(jnp.bfloat16)
         return carry
 
-    lax.fori_loop(0, wide // tile, shrink, 0)
+    lax.fori_loop(0, wide // tile, shrink, 0, unroll=2)
     acc[...] = nt(gp[...], wup[...])
 
     def norm_three(n, carry):
@@ -1058,7 +1073,7 @@
         return gain_sum, shift_sum
 
     gain_one, shift_one = lax.fori_loop(
-        0, piece // height, norm_three, (nothing, nothing), unroll=2
+        0, piece // height, norm_three, (nothing, nothing), unroll=4
     )
     side = jnp.concatenate(
         [jnp.sum(v, axis=0, keepdims=True) for v in (gain_one, shift_one, gain_two, shift_two)]
@@ -1067,6 +1082,7 @@
     ).astype(jnp.bfloat16)
 
     low = jnp.bfloat16
+    greet([there(1), there(2), there(3), by_core])
     trades = []
     for j in (3, 1, 2, 0):
         part = nt(ga[...], wout_ref[pl.ds(j * WIN, WIN), :]).astype(low)
@@ -1228,7 +1244,7 @@
         + [dma((tiles,))] * 2
         + [vm((4 * WIN, width), low)],
         compiler_params=pltpu.CompilerParams(
-            collective_id=2, has_side_effects=True, vmem_limit_bytes=62 << 20
+            collective_id=2, has_side_effects=True, vmem_limit_bytes=63 << 20
         ),
         cost_estimate=pl.CostEstimate(
             flops=2 * piece * width * (6 * wide + 3072), bytes_accessed=30 << 20, transcendentals=0
@@ -1237,12 +1253,13 @@
     )(tokens, ctx, cotangent, *norms, wout, w_up, w_down)
 
 
-def finish_kernel(share, *refs):
-    count = (len(refs) - 5) // 2
-    for n in range(count):
-        refs[count + 1 + n][...] = refs[n][...]
+def finish_kernel(share, count, *refs):
+    sources, rows_ref, dests = refs[:count], refs[count], refs[count + 1 : 2 * count + 1]
+    parts = refs[2 * count + 1 : 2 * count + 5]
+    for source, dest in zip(sources, dests):
+        dest[...] = source[...]
     seq_at = lax.axis_index("seq")
-    rows = refs[count][...]
+    rows = rows_ref[...]
     width = rows.shape[1]
     spot = lax.broadcasted_iota(jnp.int32, (width, 128), 0) - seq_at * share
     chosen = (spot == lax.broadcasted_iota(jnp.int32, (width, 128), 1)).astype(jnp.float32)
@@ -1250,16 +1267,16 @@
         rows, chosen, preferred_element_type=jnp.float32, precision=lax.Precision.HIGHEST
     )
     for n in range(4):
-        refs[2 * count + 1 + n][...] = picked[n, :share]
+        parts[n][...] = picked[n, :share]
 
 
 def finish(arrays, norm_rows, share):
-    sds = jax.ShapeDtypeStruct
+    sds, count = jax.ShapeDtypeStruct, len(arrays)
     return pl.pallas_call(
-        functools.partial(finish_kernel, share),
+        functools.partial(finish_kernel, share, count),
         out_shape=[sds(v.shape, v.dtype) for v in arrays] + [sds((share,), jnp.float32)] * 4,
-        in_specs=[VMEM] * (len(arrays) + 1),
-        out_specs=[VMEM] * (len(arrays) + 4),
+        in_specs=[VMEM] * (count + 1),
+        out_specs=[VMEM] * (count + 4),
         compiler_params=pltpu.CompilerParams(vmem_limit_bytes=62 << 20),
         name="finish",
     )(*arrays, norm_rows)
@@ -1292,7 +1309,7 @@
 
     flat = rand_blocks.reshape(1, -1)
     rand_row = jnp.pad(flat, ((0, 0), (0, 128 - flat.shape[1])))
-    keys_values, queries, stretch, context_tok, level, idx, live, wq_own, wkv_own = (
+    keys_values, queries, stretch, context_tok, level, idx, live, wq_own, wkv_own, ctx_own = (
         forward_attention(
             tokens, w_query, w_key, w_value, lengths, seq_order, rand_row, planes
         )
@@ -1308,7 +1325,13 @@
     down_pair = (down_keep.reshape(two_y), xor_swap(down_give, 1).reshape(two_y))
 
     grad_q, grad_kv = attend_back(
-        idx, live, queries, grad_ctx, level, keys_values.reshape(-1, 2 * WQ)
+        idx,
+        live,
+        queries,
+        grad_ctx,
+        ctx_own.reshape(-1, WIN),
+        level,
+        keys_values.reshape(-1, 2 * WQ),
     )
     grad_tokens, grad_wq, grad_wk, grad_wv, up_total, out_total, norm_rows, down_total = reduce_all(
         grad_kv,
@@ -1324,11 +1347,13 @@
     )
 
     finals = finish(
-        (grad_tokens, grad_wq, grad_wk, grad_wv, out_total, up_total, down_total), norm_rows, share
+        (output, grad_tokens, grad_wq, grad_wk, grad_wv, out_total, up_total, down_total),
+        norm_rows,
+        share,
     )
 
-    grad_tokens, grad_wq, grad_wk, grad_wv, grad_out, grad_up, grad_down = finals[:7]
-    gain_one, shift_one, gain_two, shift_two = finals[7:]
+    output, grad_tokens, grad_wq, grad_wk, grad_wv, grad_out, grad_up, grad_down = finals[:8]
+    gain_one, shift_one, gain_two, shift_two = finals[8:]
     return (
         output,
         grad_tokens,

time: 230 us -> 221 us (0.961)
  Pallas kernels: 223 us -> 214 us
    pallas_call x1, Pallas kernels: 62.5 us -> 58 us  [forward_attention(): pl.pallas_call(functools.partial(forward_kernel, planes), out_shape=[sds(...]
    pallas_call x1, Pallas kernels: 29.1 us -> 25 us  [attend_back(): pl.pallas_call(backward_kernel, out_shape=[jax.ShapeDtypeStruct((count, W...]
  transfers between devices with their start and end apart: 2 -> 2, of which waited for: 0 -> 2; matrix products, arithmetic and copies ran while one was open for 0% -> 0% of each run, Pallas kernels for 13% -> 11%
where the time goes in v2:
time: 221 us; the launch traced here: 220 us
  Pallas kernels  214 us (97%)
  local copies, waits for them, and re-layouts  2.38 us (1%)
    pallas_call x1, Pallas kernels, reduce_all(): pl.pallas_call(functools.partial(reduce_kernel, planes), out_shape=[sds((...  81 us
    pallas_call x1, Pallas kernels, forward_attention(): pl.pallas_call(functools.partial(forward_kernel, planes), out_shape=[sds(...  58 us
    pallas_call x1, Pallas kernels, dense_layers(): pl.pallas_call(functools.partial(dense_kernel, planes), out_shape=[sds((p...  45.2 us
    pallas_call x1, Pallas kernels, attend_back(): pl.pallas_call(backward_kernel, out_shape=[jax.ShapeDtypeStruct((count, W...  25 us
    pallas_call x1, Pallas kernels, finish(): pl.pallas_call(functools.partial(finish_kernel, share, count), out_shape=...  4.46 us
  transfers between devices with their start and end apart: 2, of which 2 were waited for; matrix products, arithmetic and copies ran while one was open for 0% of the time, Pallas kernels for 11%

profile of v2, /device:TPU:24, one launch (start us, length us, event | category | flops | bytes accessed | tf_op | source)
XLA Modules:
  0.0 220.4 jit_solution(11377495707820699414)
XLA Ops:
  0.6 0.8 copy.28
  1.4 0.1 reshape.39
  1.5 0.5 pad.4.rand_vm.rand_sm
  2.0 58.0 %forward_attention.1 = (bf16[192,64,384]{2,1,0:T(8,128)(2,1)}, bf16[2048,256]{1,0:T(8,128)(2,1)}, bf16[2048,768]{1,0:T(8,128)(2,1)}, bf16[512,1024]{1,0:T(8,128)...) custom-call(bf16[512,768]{1,0:T(8,128)(2,1)} %tok_ref.3, ...), custom_call_target="tpu_custom_call" | custom-call | flops 2013265920 | bytes 41943040 | tf_op jit(solution)/shard_map/forward_attention/pallas_call | solution.py:458
  60.1 45.2 %dense_layers.1 = (bf16[512,768]{1,0:T(8,128)(2,1)}, f32[512,768]{1,0:T(8,128)}, bf16[2048,256]{1,0:T(8,128)(2,1)}, bf16[4,48,3072]{2,1,0:T(8,128)(2,1)}, bf16[4...) custom-call(bf16[512,768]{1,0:T(8,128)(2,1)} %tok_ref.3, ...), custom_call_target="tpu_custom_call" | custom-call | flops 16911433728 | bytes 31457280 | tf_op jit(solution)/shard_map/dense_layers/pallas_call | solution.py:1209
  105.3 1.0 collective-permute-start
  106.4 0.5 collective-permute-start.1
  106.9 25.0 %attend_back.1 = (bf16[2048,256]{1,0:T(8,128)(2,1)}, bf16[12288,384]{1,0:T(8,128)(2,1)}) custom-call(s32[256]{0:T(256)} %get-tuple-element.55.idx_ref, s32[256]{0:T(256)} %get-tuple-element.56.live_ref, bf16[2048,256]{1,0:T(8,128)(2,1)} %get-tuple-element.57.q_ref, bf16[2048,256]{1,0:T(8,128)(2,1)} %get-tuple-element.58.do_ref, bf16[2048,256]{1,0:T(8,128)(2,1)} %bitcast.7, ...), custom_call_target="tpu_custom_call" | custom-call | flops 16106127360 | bytes 18874368 | tf_op jit(solution)/shard_map/attend_back/pallas_call | solution.py:504
  131.9 1.1 collective-permute-done.refs_7_
  133.0 0.0 copy-start
  133.0 0.7 collective-permute-done.1
  133.7 0.0 copy-start.1
  133.7 0.3 copy-done
  134.0 0.7 copy-done.1
  134.7 81.0 %reduce_all.1 = (f32[512,768]{1,0:T(8,128)}, f32[48,768]{1,0:T(8,128)}, f32[48,768]{1,0:T(8,128)}, f32[48,768]{1,0:T(8,128)}, f32[48,3072]{1,0:T(8,128)}, /*inde...) custom-call(bf16[12288,384]{1,0:T(8,128)(2,1)} %get-tuple-element.62.refs_0_, ...), custom_call_target="tpu_custom_call" | custom-call | flops 4026531840 | bytes 41943040 | tf_op jit(solution)/shard_map/reduce_all/pallas_call | solution.py:878
  215.7 4.5 %finish.1 = (bf16[512,768]{1,0:T(8,128)(2,1)}, f32[512,768]{1,0:T(8,128)}, f32[48,768]{1,0:T(8,128)}, f32[48,768]{1,0:T(8,128)}, f32[48,768]{1,0:T(8,128)}, /*in...) custom-call(bf16[512,768]{1,0:T(8,128)(2,1)} %get-tuple-element.54.r, ...), custom_call_target="tpu_custom_call" | custom-call | tf_op jit(solution)/shard_map/finish/pallas_call | solution.py:1275
Async XLA Ops:
  105.3 27.7 %collective-permute-start = (bf16[4,48,3072]{2,1,0:T(8,128)(2,1)}, bf16[4,48,3072]{2,1,0:T(8,128)(2,1)S(1)}, u32[]{:S(2)}, u32[]{:S(2)}) collective-permute-start(bf16[4,48,3072]{2,1,0:T(8,128)(2,1)} %get-tuple-element.69), channel_id=1, source_target_pairs={{0,4},{1,5},{2,6},{3,7},{4,0},{5,1},{6,2},{7,3},{8,12},{9,13},{10,... | collective-permute-start | bytes 3538952 | tf_op jit(solution)/shard_map/ppermute | solution.py:25
  106.4 27.3 %collective-permute-start.1 = (bf16[8,192,384]{2,1,0:T(8,128)(2,1)}, bf16[8,192,384]{2,1,0:T(8,128)(2,1)S(1)}, u32[]{:S(2)}, u32[]{:S(2)}) collective-permute-start(bf16[8,192,384]{2,1,0:T(8,128)(2,1)} %get-tuple-element.73), channel_id=1, source_target_pairs={{0,1},{1,0},{2,3},{3,2},{4,5},{5,4},{6,7},{7,6},{8,9},{9,8},{10,11... | collective-permute-start | bytes 3538952 | tf_op jit(solution)/shard_map/ppermute | solution.py:25
  133.0 1.0 copy-start
  133.7 1.0 copy-start.1

commit v3 on v2

--- a/solution.py
+++ b/solution.py
@@ -105,7 +105,7 @@
             acc[at, 256:384] += v_s[:, 128:]
         return carry
 
-    lax.fori_loop(0, q_ref.shape[0] // BLK, step, 0, unroll=4)
+    lax.fori_loop(0, q_ref.shape[0] // BLK, step, 0, unroll=8)
 
     def emit(n, carry):
         at = pl.ds(pl.multiple_of(n * 256, 256), 256)
@@ -169,8 +169,7 @@
         row = x_of * per + near
         draws = []
         for n in range(SLOTS - 5):
-            spot = row * (SLOTS - 5) + n
-            draw = jnp.where(far >= 2, rand_got[0, spot], rand_own[0, spot])
+            draw = jnp.where(far >= 2, rand_got[row, n], rand_own[row, n])
             for power in range(16, -1, -1):
                 multiple = span * (1 << power)
                 draw = jnp.where(draw >= multiple, draw - multiple, draw)
@@ -576,6 +575,21 @@
     def to_owner(j):
         return remote(dx_out.at[j - 1], dx_in.at[j - 1], x_s, x_r, j - 1, there(j))
 
+    half_piece = piece // 2
+
+    def pass_on(j):
+        span = pl.ds((j - 1) * half_piece, half_piece)
+        return remote(dx_out.at[2, span], dx_in.at[2, span], x_s, x_r, 1 + j, there(j))
+
+    def take_in(j):
+        span = pl.ds((j - 1) * half_piece, half_piece)
+        pass_on(j).wait_recv()
+        spot = 2 - j
+        dx_out[spot, span, :] = (
+            dx_out[spot, span, :].astype(f32) + dx_in[2, span, :].astype(f32)
+        ).astype(low)
+        to_owner(3 - j).start()
+
     def every(n, action):
         j = 3 - n
         for turn, r in ((n * 2, 0), (n * 2 + 1, 2)):
@@ -618,13 +632,13 @@
         j = 3 - n
         z_out[chunk(0, j), :] = both(2 * n, 0, j).astype(low)
 
-        @pl.when(has_below)
+        @pl.when(jnp.logical_and(has_below, n < 3))
         def _():
             to_below(j).start()
 
         z_out[chunk(part, j), :] = both(2 * n + 1, 2, j).astype(low)
 
-        @pl.when(has_above)
+        @pl.when(jnp.logical_and(has_above, n < 3))
         def _():
             to_above(j).start()
 
@@ -681,14 +695,16 @@
     def outer(j):
         acc[...] += tn(xs[chunk(0, j), :], g_all[...])
 
-    def send_back(n, carry):
+    def turn_back(n, carry):
         arrive(n)
         dx_out[2 - n] = back(3 - n).astype(low)
-        to_owner(3 - n).start()
         outer(3 - n)
         return carry
 
-    lax.fori_loop(0, 3, send_back, 0)
+    turn_back(0, 0)
+    pass_on(1).start()
+    pass_on(2).start()
+    turn_back(1, 0)
 
     for n in range(3):
         w2[n].wait_recv()
@@ -735,8 +751,22 @@
                     ).astype(low)
                     line_copy(n, way, t).start()
 
+    line_step(0)
+
+    @pl.when(has_below)
+    def _():
+        to_below(0).start()
+
+    @pl.when(has_above)
+    def _():
+        to_above(0).start()
+
+    take_in(1)
+    turn_back(2, 0)
+    take_in(2)
+    if planes > 2:
+        line_step(1)
     arrive(3)
-    line_step(0)
     tok_out[...] = one[...] + back(0)
     outer(0)
 
@@ -749,8 +779,6 @@
                 p_slab[k, p, y] = acc[at : at + share, :].astype(low)
     pk = remote(p_slab.at[1 - core], p_core, pk_s, pk_r, 0, by_core)
     pk.start()
-    if planes > 2:
-        line_step(1)
     pk.wait_recv()
 
     def merge_core(p, carry):
@@ -793,7 +821,7 @@
         w4.append(remote(fin[n].at[x_at], fin[n].at[x_at], w4_s, w4_r, n, by_x))
         w4[n].start()
 
-    for j in (3, 2, 1):
+    for j in (2, 1):
         to_owner(j).wait_recv()
         tok_out[...] += dx_in[j - 1].astype(f32)
 
@@ -846,8 +874,9 @@
         return carry
 
     lax.fori_loop(0, 4, settle, 0)
-    for j in (1, 2, 3):
+    for j in (1, 2):
         to_owner(j).wait_send()
+        pass_on(j).wait_send()
 
     def settle_line(t, carry):
         for n in range(3):
@@ -914,8 +943,7 @@
         + [vm((2, rest) + k, low) for k in kinds] * 2
         + [dma((12,)), dma((11,))]
         + [dma((12,))] * 2
-        + [dma((4,))] * 4
-        + [dma((3,))] * 2
+        + [dma((4,))] * 6
         + [dma((1,))] * 2
         + [dma((rest,))] * 2
         + [dma((3,))] * 2
@@ -1020,12 +1048,12 @@
         at = cols_of(n)
         pre = jnp.dot(nl[...], wup[:, at], preferred_element_type=f32)
         square = pre * pre
-        inner = 0.7978845608028654 * pre * (1.0 + 0.044715 * square)
-        bend = jnp.tanh(inner)
+        bend = jnp.tanh(pre * (0.7978845608028654 + 0.035677408136300125 * square))
         half_up = 0.5 + 0.5 * bend
-        hid[:, at] = (pre * half_up).astype(jnp.bfloat16)
-        slope[:, at] = half_up + 0.5 * pre * (1.0 - bend * bend) * (
-            0.7978845608028654 + 0.1070322243 * square
+        value = pre * half_up
+        hid[:, at] = value.astype(jnp.bfloat16)
+        slope[:, at] = half_up + value * (1.0 - bend) * (
+            0.7978845608028654 + 0.10703222440890037 * square
         )
         return carry
 
@@ -1132,6 +1160,29 @@
         return carry
 
     lax.fori_loop(0, tiles, make_up, 0)
+    moved = []
+
+    def move(source, dest):
+        moved.append(pltpu.make_async_copy(source, dest, mv_sem.at[len(moved)]))
+        moved[-1].start()
+
+    half = width // 2
+
+    def sum_down(t, carry):
+        down_copy(t).wait_recv()
+        for n in range(per):
+            q = t * per + n
+            total = (
+                down_loc[core, q].astype(jnp.float32) + down_got[q].astype(jnp.float32)
+            ).astype(low)
+            down_sum[0, q] = total[:, :half]
+            down_sum[1, q] = total[:, half:]
+        return carry
+
+    lax.fori_loop(0, tiles, sum_down, 0)
+    move(down_sum.at[x_at], down_keep)
+    move(down_sum.at[1 - x_at], down_give)
+
     per_group = pairs // 4
     for j in range(4):
         cell = tn(ctx_ref[:, j * WIN : (j + 1) * WIN], ga[...])
@@ -1144,29 +1195,6 @@
             out_loc[k, q, share:, :] = side
     outs = remote(out_loc.at[1 - core], out_got, out_s, out_r, 0, by_core)
     outs.start()
-
-    moved = []
-
-    def move(source, dest):
-        moved.append(pltpu.make_async_copy(source, dest, mv_sem.at[len(moved)]))
-        moved[-1].start()
-
-    half = width // 2
-
-    def sum_down(t, carry):
-        down_copy(t).wait_recv()
-        for n in range(per):
-            q = t * per + n
-            total = (
-                down_loc[core, q].astype(jnp.float32) + down_got[q].astype(jnp.float32)
-            ).astype(low)
-            down_sum[0, q] = total[:, :half]
-            down_sum[1, q] = total[:, half:]
-        return carry
-
-    lax.fori_loop(0, tiles, sum_down, 0)
-    move(down_sum.at[x_at], down_keep)
-    move(down_sum.at[1 - x_at], down_give)
 
     def sum_up(q, carry):
         up_got[q] = (up_loc[core, q].astype(jnp.float32) + up_got[q].astype(jnp.float32)).astype(low)
@@ -1307,11 +1335,9 @@
     plane, y_at, core = seq_at // 4, (seq_at // 2) % 2, seq_at % 2
     group = y_at * 2 + x_at
 
-    flat = rand_blocks.reshape(1, -1)
-    rand_row = jnp.pad(flat, ((0, 0), (0, 128 - flat.shape[1])))
     keys_values, queries, stretch, context_tok, level, idx, live, wq_own, wkv_own, ctx_own = (
         forward_attention(
-            tokens, w_query, w_key, w_value, lengths, seq_order, rand_row, planes
+            tokens, w_query, w_key, w_value, lengths, seq_order, rand_blocks, planes
         )
     )
     share = width // seqs

time: 221 us -> 220 us (level)
  Pallas kernels: 214 us -> 211 us
where the time goes in v3:
time: 220 us; the launch traced here: 219 us
  Pallas kernels  211 us (96%)
  waiting for transfers between devices  2.63 us (1%)
  local copies, waits for them, and re-layouts  2.37 us (1%)
    pallas_call x1, Pallas kernels, reduce_all(): pl.pallas_call(functools.partial(reduce_kernel, planes), out_shape=[sds((...  79.5 us
    pallas_call x1, Pallas kernels, forward_attention(): pl.pallas_call(functools.partial(forward_kernel, planes), out_shape=[sds(...  58.1 us
    pallas_call x1, Pallas kernels, dense_layers(): pl.pallas_call(functools.partial(dense_kernel, planes), out_shape=[sds((p...  45.2 us
    pallas_call x1, Pallas kernels, attend_back(): pl.pallas_call(backward_kernel, out_shape=[jax.ShapeDtypeStruct((count, W...  24 us
    pallas_call x1, Pallas kernels, finish(): pl.pallas_call(functools.partial(finish_kernel, share, count), out_shape=...  4.46 us
  transfers between devices with their start and end apart: 2, of which 2 were waited for; matrix products, arithmetic and copies ran while one was open for 0% of the time, Pallas kernels for 11%

profile of v3, /device:TPU:24, one launch (start us, length us, event | category | flops | bytes accessed | tf_op | source)
XLA Modules:
  0.0 218.8 jit_solution(2970392019447794968)
XLA Ops:
  0.6 1.4 copy.27.rand_vm.rand_sm
  2.0 58.1 %forward_attention.1 = (bf16[192,64,384]{2,1,0:T(8,128)(2,1)}, bf16[2048,256]{1,0:T(8,128)(2,1)}, bf16[2048,768]{1,0:T(8,128)(2,1)}, bf16[512,1024]{1,0:T(8,128)...) custom-call(bf16[512,768]{1,0:T(8,128)(2,1)} %tok_ref.3, ...), custom_call_target="tpu_custom_call" | custom-call | flops 2013265920 | bytes 41943040 | tf_op jit(solution)/shard_map/forward_attention/pallas_call | solution.py:457
  60.1 45.2 %dense_layers.1 = (bf16[512,768]{1,0:T(8,128)(2,1)}, f32[512,768]{1,0:T(8,128)}, bf16[2048,256]{1,0:T(8,128)(2,1)}, bf16[4,48,3072]{2,1,0:T(8,128)(2,1)}, bf16[4...) custom-call(bf16[512,768]{1,0:T(8,128)(2,1)} %tok_ref.3, ...), custom_call_target="tpu_custom_call" | custom-call | flops 16911433728 | bytes 31457280 | tf_op jit(solution)/shard_map/dense_layers/pallas_call | solution.py:1237
  105.3 1.2 collective-permute-start
  106.5 0.5 collective-permute-start.1
  107.0 24.0 %attend_back.1 = (bf16[2048,256]{1,0:T(8,128)(2,1)}, bf16[12288,384]{1,0:T(8,128)(2,1)}) custom-call(s32[256]{0:T(256)} %get-tuple-element.55.idx_ref, s32[256]{0:T(256)} %get-tuple-element.56.live_ref, bf16[2048,256]{1,0:T(8,128)(2,1)} %get-tuple-element.57.q_ref, bf16[2048,256]{1,0:T(8,128)(2,1)} %get-tuple-element.58.do_ref, bf16[2048,256]{1,0:T(8,128)(2,1)} %bitcast.7, ...), custom_call_target="tpu_custom_call" | custom-call | flops 16106127360 | bytes 18874368 | tf_op jit(solution)/shard_map/attend_back/pallas_call | solution.py:503
  131.0 1.8 collective-permute-done.refs_7_
  132.8 0.0 copy-start
  132.9 0.8 collective-permute-done.1
  133.7 0.0 copy-start.1
  133.7 0.2 copy-done
  133.9 0.8 copy-done.1
  134.7 79.5 %reduce_all.1 = (f32[512,768]{1,0:T(8,128)}, f32[48,768]{1,0:T(8,128)}, f32[48,768]{1,0:T(8,128)}, f32[48,768]{1,0:T(8,128)}, f32[48,3072]{1,0:T(8,128)}, /*inde...) custom-call(bf16[12288,384]{1,0:T(8,128)(2,1)} %get-tuple-element.62.refs_0_, ...), custom_call_target="tpu_custom_call" | custom-call | flops 4026531840 | bytes 41943040 | tf_op jit(solution)/shard_map/reduce_all/pallas_call | solution.py:907
  214.2 4.5 %finish.1 = (bf16[512,768]{1,0:T(8,128)(2,1)}, f32[512,768]{1,0:T(8,128)}, f32[48,768]{1,0:T(8,128)}, f32[48,768]{1,0:T(8,128)}, f32[48,768]{1,0:T(8,128)}, /*in...) custom-call(bf16[512,768]{1,0:T(8,128)(2,1)} %get-tuple-element.54.r, ...), custom_call_target="tpu_custom_call" | custom-call | tf_op jit(solution)/shard_map/finish/pallas_call | solution.py:1303
Async XLA Ops:
  105.3 27.6 %collective-permute-start = (bf16[4,48,3072]{2,1,0:T(8,128)(2,1)}, bf16[4,48,3072]{2,1,0:T(8,128)(2,1)S(1)}, u32[]{:S(2)}, u32[]{:S(2)}) collective-permute-start(bf16[4,48,3072]{2,1,0:T(8,128)(2,1)} %get-tuple-element.69), channel_id=1, source_target_pairs={{0,4},{1,5},{2,6},{3,7},{4,0},{5,1},{6,2},{7,3},{8,12},{9,13},{10,... | collective-permute-start | bytes 3538952 | tf_op jit(solution)/shard_map/ppermute | solution.py:25
  106.5 27.2 %collective-permute-start.1 = (bf16[8,192,384]{2,1,0:T(8,128)(2,1)}, bf16[8,192,384]{2,1,0:T(8,128)(2,1)S(1)}, u32[]{:S(2)}, u32[]{:S(2)}) collective-permute-start(bf16[8,192,384]{2,1,0:T(8,128)(2,1)} %get-tuple-element.73), channel_id=1, source_target_pairs={{0,1},{1,0},{2,3},{3,2},{4,5},{5,4},{6,7},{7,6},{8,9},{9,8},{10,11... | collective-permute-start | bytes 3538952 | tf_op jit(solution)/shard_map/ppermute | solution.py:25
  132.8 1.0 copy-start
  133.7 1.0 copy-start.1

commit v4 on v3

--- a/solution.py
+++ b/solution.py
@@ -169,7 +169,7 @@
         row = x_of * per + near
         draws = []
         for n in range(SLOTS - 5):
-            draw = jnp.where(far >= 2, rand_got[row, n], rand_own[row, n])
+            draw = jnp.where(far >= 2, rand_got[n, row], rand_own[n, row])
             for power in range(16, -1, -1):
                 multiple = span * (1 << power)
                 draw = jnp.where(draw >= multiple, draw - multiple, draw)
@@ -510,7 +510,7 @@
             pltpu.VMEM((6 * rows, width), jnp.float32),
             pltpu.SemaphoreType.DMA((1,)),
         ],
-        compiler_params=pltpu.CompilerParams(vmem_limit_bytes=56 << 20),
+        compiler_params=pltpu.CompilerParams(vmem_limit_bytes=62 << 20),
         cost_estimate=pl.CostEstimate(
             flops=2 * 10 * count * 3 * 256 * 512, bytes_accessed=24 * rows * width, transcendentals=count * 3 * 512
         ),
@@ -767,7 +767,6 @@
     if planes > 2:
         line_step(1)
     arrive(3)
-    tok_out[...] = one[...] + back(0)
     outer(0)
 
     share = p_slab.shape[3]
@@ -779,6 +778,7 @@
                 p_slab[k, p, y] = acc[at : at + share, :].astype(low)
     pk = remote(p_slab.at[1 - core], p_core, pk_s, pk_r, 0, by_core)
     pk.start()
+    tok_out[...] = one[...] + back(0)
     pk.wait_recv()
 
     def merge_core(p, carry):
@@ -1284,8 +1284,14 @@
 def finish_kernel(share, count, *refs):
     sources, rows_ref, dests = refs[:count], refs[count], refs[count + 1 : 2 * count + 1]
     parts = refs[2 * count + 1 : 2 * count + 5]
-    for source, dest in zip(sources, dests):
-        dest[...] = source[...]
+    held, sems = refs[2 * count + 5 : 3 * count + 5], refs[3 * count + 5]
+    reads = [pltpu.make_async_copy(sources[n], held[n], sems.at[0, n]) for n in range(count)]
+    writes = [pltpu.make_async_copy(held[n], dests[n], sems.at[1, n]) for n in range(count)]
+    for copy in reads:
+        copy.start()
+    for n in range(count):
+        reads[n].wait()
+        writes[n].start()
     seq_at = lax.axis_index("seq")
     rows = rows_ref[...]
     width = rows.shape[1]
@@ -1296,6 +1302,8 @@
     )
     for n in range(4):
         parts[n][...] = picked[n, :share]
+    for copy in writes:
+        copy.wait()
 
 
 def finish(arrays, norm_rows, share):
@@ -1303,8 +1311,10 @@
     return pl.pallas_call(
         functools.partial(finish_kernel, share, count),
         out_shape=[sds(v.shape, v.dtype) for v in arrays] + [sds((share,), jnp.float32)] * 4,
-        in_specs=[VMEM] * (count + 1),
-        out_specs=[VMEM] * (count + 4),
+        in_specs=[ANY] * count + [VMEM],
+        out_specs=[ANY] * count + [VMEM] * 4,
+        scratch_shapes=[pltpu.VMEM(v.shape, v.dtype) for v in arrays]
+        + [pltpu.SemaphoreType.DMA((2, count))],
         compiler_params=pltpu.CompilerParams(vmem_limit_bytes=62 << 20),
         name="finish",
     )(*arrays, norm_rows)
@@ -1337,7 +1347,7 @@
 
     keys_values, queries, stretch, context_tok, level, idx, live, wq_own, wkv_own, ctx_own = (
         forward_attention(
-            tokens, w_query, w_key, w_value, lengths, seq_order, rand_blocks, planes
+            tokens, w_query, w_key, w_value, lengths, seq_order, rand_blocks.T, planes
         )
     )
     share = width // seqs

time: 220 us -> 218 us (level)
  no operation moved by 1% of the time
where the time goes in v4:
time: 218 us; the launch traced here: 217 us
  Pallas kernels  212 us (97%)
  waiting for transfers between devices  2.75 us (1%)
    pallas_call x1, Pallas kernels, reduce_all(): pl.pallas_call(functools.partial(reduce_kernel, planes), out_shape=[sds((...  79.6 us
    pallas_call x1, Pallas kernels, forward_attention(): pl.pallas_call(functools.partial(forward_kernel, planes), out_shape=[sds(...  58 us
    pallas_call x1, Pallas kernels, dense_layers(): pl.pallas_call(functools.partial(dense_kernel, planes), out_shape=[sds((p...  45.2 us
    pallas_call x1, Pallas kernels, attend_back(): pl.pallas_call(backward_kernel, out_shape=[jax.ShapeDtypeStruct((count, W...  24 us
    pallas_call x1, Pallas kernels, finish(): pl.pallas_call(functools.partial(finish_kernel, share, count), out_shape=...  4.78 us
  transfers between devices with their start and end apart: 2, of which 2 were waited for; matrix products, arithmetic and copies ran while one was open for 0% of the time, Pallas kernels for 11%

profile of v4, /device:TPU:24, one launch (start us, length us, event | category | flops | bytes accessed | tf_op | source)
XLA Modules:
  0.0 217.0 jit_solution(5574936316623580659)
XLA Ops:
  0.6 58.0 %forward_attention.1 = (bf16[192,64,384]{2,1,0:T(8,128)(2,1)}, bf16[2048,256]{1,0:T(8,128)(2,1)}, bf16[2048,768]{1,0:T(8,128)(2,1)}, bf16[512,1024]{1,0:T(8,128)...) custom-call(bf16[512,768]{1,0:T(8,128)(2,1)} %tok_ref.3, ...), custom_call_target="tpu_custom_call" | custom-call | flops 2013265920 | bytes 41943040 | tf_op jit(solution)/shard_map/forward_attention/pallas_call | solution.py:457
  58.6 45.2 %dense_layers.1 = (bf16[512,768]{1,0:T(8,128)(2,1)}, f32[512,768]{1,0:T(8,128)}, bf16[2048,256]{1,0:T(8,128)(2,1)}, bf16[4,48,3072]{2,1,0:T(8,128)(2,1)}, bf16[4...) custom-call(bf16[512,768]{1,0:T(8,128)(2,1)} %tok_ref.3, ...), custom_call_target="tpu_custom_call" | custom-call | flops 16911433728 | bytes 31457280 | tf_op jit(solution)/shard_map/dense_layers/pallas_call | solution.py:1237
  103.8 1.1 collective-permute-start
  104.9 0.5 collective-permute-start.1
  105.4 24.0 %attend_back.1 = (bf16[2048,256]{1,0:T(8,128)(2,1)}, bf16[12288,384]{1,0:T(8,128)(2,1)}) custom-call(s32[256]{0:T(256)} %get-tuple-element.55.idx_ref, s32[256]{0:T(256)} %get-tuple-element.56.live_ref, bf16[2048,256]{1,0:T(8,128)(2,1)} %get-tuple-element.57.q_ref, bf16[2048,256]{1,0:T(8,128)(2,1)} %get-tuple-element.58.do_ref, bf16[2048,256]{1,0:T(8,128)(2,1)} %bitcast.9, ...), custom_call_target="tpu_custom_call" | custom-call | flops 16106127360 | bytes 18874368 | tf_op jit(solution)/shard_map/attend_back/pallas_call | solution.py:503
  129.4 1.9 collective-permute-done.refs_7_
  131.4 0.0 copy-start
  131.4 0.8 collective-permute-done.1
  132.2 0.2 copy-done
  132.4 79.6 %reduce_all.1 = (f32[512,768]{1,0:T(8,128)}, f32[48,768]{1,0:T(8,128)}, f32[48,768]{1,0:T(8,128)}, f32[48,768]{1,0:T(8,128)}, f32[48,3072]{1,0:T(8,128)}, /*inde...) custom-call(bf16[12288,384]{1,0:T(8,128)(2,1)} %get-tuple-element.62.refs_0_, ...), custom_call_target="tpu_custom_call" | custom-call | flops 4026531840 | bytes 41943040 | tf_op jit(solution)/shard_map/reduce_all/pallas_call | solution.py:907
  212.0 4.8 %finish.1 = (bf16[512,768]{1,0:T(8,128)(2,1)}, f32[512,768]{1,0:T(8,128)}, f32[48,768]{1,0:T(8,128)}, f32[48,768]{1,0:T(8,128)}, f32[48,768]{1,0:T(8,128)}, /*in...) custom-call(bf16[512,768]{1,0:T(8,128)(2,1)} %get-tuple-element.54.r, ...), custom_call_target="tpu_custom_call" | custom-call | tf_op jit(solution)/shard_map/finish/pallas_call | solution.py:1311
Async XLA Ops:
  103.8 27.5 %collective-permute-start = (bf16[4,48,3072]{2,1,0:T(8,128)(2,1)}, bf16[4,48,3072]{2,1,0:T(8,128)(2,1)S(1)}, u32[]{:S(2)}, u32[]{:S(2)}) collective-permute-start(bf16[4,48,3072]{2,1,0:T(8,128)(2,1)} %get-tuple-element.69), channel_id=1, source_target_pairs={{0,4},{1,5},{2,6},{3,7},{4,0},{5,1},{6,2},{7,3},{8,12},{9,13},{10,... | collective-permute-start | bytes 3538952 | tf_op jit(solution)/shard_map/ppermute | solution.py:25
  104.9 27.3 %collective-permute-start.1 = (bf16[8,192,384]{2,1,0:T(8,128)(2,1)}, bf16[8,192,384]{2,1,0:T(8,128)(2,1)}, u32[]{:S(2)}, u32[]{:S(2)}) collective-permute-start(bf16[8,192,384]{2,1,0:T(8,128)(2,1)} %get-tuple-element.73), channel_id=1, source_target_pairs={{0,1},{1,0},{2,3},{3,2},{4,5},{5,4},{6,7},{7,6},{8,9},{9,8},{10,11... | collective-permute-start | bytes 3538952 | tf_op jit(solution)/shard_map/ppermute | solution.py:25
  131.4 1.0 copy-start

commit v5 on v4

--- a/solution.py
+++ b/solution.py
@@ -825,6 +825,41 @@
         to_owner(j).wait_recv()
         tok_out[...] += dx_in[j - 1].astype(f32)
 
+    for copy in list(w2.values()) + [pk]:
+        copy.wait_send()
+
+    def settle(n, carry):
+        every(n, lambda turn, r, j: to_core(turn, r, j).wait_send())
+        to_core(8 + n, 1, 3 - n).wait_send()
+
+        @pl.when(has_below)
+        def _():
+            to_below(3 - n).wait_send()
+
+        @pl.when(has_above)
+        def _():
+            to_above(3 - n).wait_send()
+
+        return carry
+
+    lax.fori_loop(0, 4, settle, 0)
+    for j in (1, 2):
+        to_owner(j).wait_send()
+        pass_on(j).wait_send()
+
+    def settle_line(t, carry):
+        for n in range(3):
+            for way in range(2):
+                spot = (planes - 1 - plane) if way else plane
+
+                @pl.when(jnp.logical_and(t >= spot, spot < planes - 1))
+                def _():
+                    line_copy(n, way, t).wait_send()
+
+        return carry
+
+    lax.fori_loop(0, planes - 1, settle_line, 0)
+
     total = p_z[plane].astype(f32)
     for g in range(1, planes):
         pz[g - 1].wait_recv()
@@ -838,12 +873,6 @@
         copy.start()
     p_all[0] = p_fin[y_at]
 
-    for copy in pf:
-        copy.wait()
-    for a in range(4):
-        grads = p_all[a ^ group].astype(f32)
-        for n, dest in enumerate((k_out, v_out, q_out)):
-            dest[:, a * WQ : (a + 1) * WQ] = grads[:, n * WQ : (n + 1) * WQ]
     for n, dest in ((0, up_out), (2, down_out)):
         w4[n].wait()
         width = dest.shape[1] // 2
@@ -856,40 +885,14 @@
         side_out[:, side * width : (side + 1) * width] = done[:share]
         norm_out[:, side * width : (side + 1) * width] = done[share : share + 8]
 
-    for copy in list(w2.values()) + pz + [pk]:
+    for copy in pf:
+        copy.wait()
+    for a in range(4):
+        grads = p_all[a ^ group].astype(f32)
+        for n, dest in enumerate((k_out, v_out, q_out)):
+            dest[:, a * WQ : (a + 1) * WQ] = grads[:, n * WQ : (n + 1) * WQ]
+    for copy in pz:
         copy.wait_send()
-
-    def settle(n, carry):
-        every(n, lambda turn, r, j: to_core(turn, r, j).wait_send())
-        to_core(8 + n, 1, 3 - n).wait_send()
-
-        @pl.when(has_below)
-        def _():
-            to_below(3 - n).wait_send()
-
-        @pl.when(has_above)
-        def _():
-            to_above(3 - n).wait_send()
-
-        return carry
-
-    lax.fori_loop(0, 4, settle, 0)
-    for j in (1, 2):
-        to_owner(j).wait_send()
-        pass_on(j).wait_send()
-
-    def settle_line(t, carry):
-        for n in range(3):
-            for way in range(2):
-                spot = (planes - 1 - plane) if way else plane
-
-                @pl.when(jnp.logical_and(t >= spot, spot < planes - 1))
-                def _():
-                    line_copy(n, way, t).wait_send()
-
-        return carry
-
-    lax.fori_loop(0, planes - 1, settle_line, 0)
 
 
 def reduce_all(dkv, dq, stretch, wq, wkv, one, up, out, down, planes):
@@ -1045,7 +1048,7 @@
     bring[0].wait()
 
     def expand(n, carry):
-        at = cols_of(n)
+        at = pl.ds(pl.multiple_of(n * 768, 768), 768)
         pre = jnp.dot(nl[...], wup[:, at], preferred_element_type=f32)
         square = pre * pre
         bend = jnp.tanh(pre * (0.7978845608028654 + 0.035677408136300125 * square))
@@ -1057,7 +1060,7 @@
         )
         return carry
 
-    lax.fori_loop(0, wide // tile, expand, 0, unroll=2)
+    lax.fori_loop(0, wide // 768, expand, 0)
     bring[1].wait()
     acc[...] = jnp.dot(hid[...], wdown[...], preferred_element_type=f32)
     nothing = jnp.zeros((8, width), f32)

time: 218 us -> 217 us (level)
  no operation moved by 1% of the time
where the time goes in v5:
time: 217 us; the launch traced here: 216 us
  Pallas kernels  211 us (97%)
  waiting for transfers between devices  2.74 us (1%)
    pallas_call x1, Pallas kernels, reduce_all(): pl.pallas_call(functools.partial(reduce_kernel, planes), out_shape=[sds((...  79.4 us
    pallas_call x1, Pallas kernels, forward_attention(): pl.pallas_call(functools.partial(forward_kernel, planes), out_shape=[sds(...  58 us
    pallas_call x1, Pallas kernels, dense_layers(): pl.pallas_call(functools.partial(dense_kernel, planes), out_shape=[sds((p...  44.4 us
    pallas_call x1, Pallas kernels, attend_back(): pl.pallas_call(backward_kernel, out_shape=[jax.ShapeDtypeStruct((count, W...  24 us
    pallas_call x1, Pallas kernels, finish(): pl.pallas_call(functools.partial(finish_kernel, share, count), out_shape=...  4.78 us
  transfers between devices with their start and end apart: 2, of which 2 were waited for; matrix products, arithmetic and copies ran while one was open for 0% of the time, Pallas kernels for 11%

profile of v5, /device:TPU:24, one launch (start us, length us, event | category | flops | bytes accessed | tf_op | source)
XLA Modules:
  0.0 216.0 jit_solution(418816559035939005)
XLA Ops:
  0.6 58.0 %forward_attention.1 = (bf16[192,64,384]{2,1,0:T(8,128)(2,1)}, bf16[2048,256]{1,0:T(8,128)(2,1)}, bf16[2048,768]{1,0:T(8,128)(2,1)}, bf16[512,1024]{1,0:T(8,128)...) custom-call(bf16[512,768]{1,0:T(8,128)(2,1)} %tok_ref.3, ...), custom_call_target="tpu_custom_call" | custom-call | flops 2013265920 | bytes 41943040 | tf_op jit(solution)/shard_map/forward_attention/pallas_call | solution.py:457
  58.6 44.4 %dense_layers.1 = (bf16[512,768]{1,0:T(8,128)(2,1)}, f32[512,768]{1,0:T(8,128)}, bf16[2048,256]{1,0:T(8,128)(2,1)}, bf16[4,48,3072]{2,1,0:T(8,128)(2,1)}, bf16[4...) custom-call(bf16[512,768]{1,0:T(8,128)(2,1)} %tok_ref.3, ...), custom_call_target="tpu_custom_call" | custom-call | flops 16911433728 | bytes 31457280 | tf_op jit(solution)/shard_map/dense_layers/pallas_call | solution.py:1240
  103.1 1.1 collective-permute-start
  104.1 0.5 collective-permute-start.1
  104.7 24.0 %attend_back.1 = (bf16[2048,256]{1,0:T(8,128)(2,1)}, bf16[12288,384]{1,0:T(8,128)(2,1)}) custom-call(s32[256]{0:T(256)} %get-tuple-element.55.idx_ref, s32[256]{0:T(256)} %get-tuple-element.56.live_ref, bf16[2048,256]{1,0:T(8,128)(2,1)} %get-tuple-element.57.q_ref, bf16[2048,256]{1,0:T(8,128)(2,1)} %get-tuple-element.58.do_ref, bf16[2048,256]{1,0:T(8,128)(2,1)} %bitcast.9, ...), custom_call_target="tpu_custom_call" | custom-call | flops 16106127360 | bytes 18874368 | tf_op jit(solution)/shard_map/attend_back/pallas_call | solution.py:503
  128.6 1.9 collective-permute-done.refs_7_
  130.6 0.0 copy-start
  130.6 0.8 collective-permute-done.1
  131.4 0.2 copy-done
  131.6 79.4 %reduce_all.1 = (f32[512,768]{1,0:T(8,128)}, f32[48,768]{1,0:T(8,128)}, f32[48,768]{1,0:T(8,128)}, f32[48,768]{1,0:T(8,128)}, f32[48,3072]{1,0:T(8,128)}, /*inde...) custom-call(bf16[12288,384]{1,0:T(8,128)(2,1)} %get-tuple-element.62.refs_0_, ...), custom_call_target="tpu_custom_call" | custom-call | flops 4026531840 | bytes 41943040 | tf_op jit(solution)/shard_map/reduce_all/pallas_call | solution.py:910
  211.1 4.8 %finish.1 = (bf16[512,768]{1,0:T(8,128)(2,1)}, f32[512,768]{1,0:T(8,128)}, f32[48,768]{1,0:T(8,128)}, f32[48,768]{1,0:T(8,128)}, f32[48,768]{1,0:T(8,128)}, /*in...) custom-call(bf16[512,768]{1,0:T(8,128)(2,1)} %get-tuple-element.54.r, ...), custom_call_target="tpu_custom_call" | custom-call | tf_op jit(solution)/shard_map/finish/pallas_call | solution.py:1314
Async XLA Ops:
  103.1 27.5 %collective-permute-start = (bf16[4,48,3072]{2,1,0:T(8,128)(2,1)}, bf16[4,48,3072]{2,1,0:T(8,128)(2,1)S(1)}, u32[]{:S(2)}, u32[]{:S(2)}) collective-permute-start(bf16[4,48,3072]{2,1,0:T(8,128)(2,1)} %get-tuple-element.69), channel_id=1, source_target_pairs={{0,4},{1,5},{2,6},{3,7},{4,0},{5,1},{6,2},{7,3},{8,12},{9,13},{10,... | collective-permute-start | bytes 3538952 | tf_op jit(solution)/shard_map/ppermute | solution.py:25
  104.1 27.3 %collective-permute-start.1 = (bf16[8,192,384]{2,1,0:T(8,128)(2,1)}, bf16[8,192,384]{2,1,0:T(8,128)(2,1)}, u32[]{:S(2)}, u32[]{:S(2)}) collective-permute-start(bf16[8,192,384]{2,1,0:T(8,128)(2,1)} %get-tuple-element.73), channel_id=1, source_target_pairs={{0,1},{1,0},{2,3},{3,2},{4,5},{5,4},{6,7},{7,6},{8,9},{9,8},{10,11... | collective-permute-start | bytes 3538952 | tf_op jit(solution)/shard_map/ppermute | solution.py:25
  130.6 1.0 copy-start

commit v6 on v5

--- a/solution.py
+++ b/solution.py
@@ -1084,12 +1084,12 @@
     gain_two, shift_two = lax.fori_loop(0, piece // height, norm_two, (nothing, nothing), unroll=4)
 
     def shrink(n, carry):
-        at = cols_of(n)
+        at = pl.ds(pl.multiple_of(n * 768, 768), 768)
         back = nt(gm[...], wdown[at, :])
         gp[:, at] = (back * slope[:, at]).astype(jnp.bfloat16)
         return carry
 
-    lax.fori_loop(0, wide // tile, shrink, 0, unroll=2)
+    lax.fori_loop(0, wide // 768, shrink, 0)
     acc[...] = nt(gp[...], wup[...])
 
     def norm_three(n, carry):

time: 217 us -> 216 us (level)
  no operation moved by 1% of the time
where the time goes in v6:
time: 216 us; the launch traced here: 215 us
  Pallas kernels  210 us (97%)
  waiting for transfers between devices  2.73 us (1%)
    pallas_call x1, Pallas kernels, reduce_all(): pl.pallas_call(functools.partial(reduce_kernel, planes), out_shape=[sds((...  79.4 us
    pallas_call x1, Pallas kernels, forward_attention(): pl.pallas_call(functools.partial(forward_kernel, planes), out_shape=[sds(...  58 us
    pallas_call x1, Pallas kernels, dense_layers(): pl.pallas_call(functools.partial(dense_kernel, planes), out_shape=[sds((p...  43.7 us
    pallas_call x1, Pallas kernels, attend_back(): pl.pallas_call(backward_kernel, out_shape=[jax.ShapeDtypeStruct((count, W...  24 us
    pallas_call x1, Pallas kernels, finish(): pl.pallas_call(functools.partial(finish_kernel, share, count), out_shape=...  4.78 us
  transfers between devices with their start and end apart: 2, of which 2 were waited for; matrix products, arithmetic and copies ran while one was open for 0% of the time, Pallas kernels for 11%

profile of v6, /device:TPU:24, one launch (start us, length us, event | category | flops | bytes accessed | tf_op | source)
XLA Modules:
  0.0 215.3 jit_solution(9130271523782425659)
XLA Ops:
  0.6 58.0 %forward_attention.1 = (bf16[192,64,384]{2,1,0:T(8,128)(2,1)}, bf16[2048,256]{1,0:T(8,128)(2,1)}, bf16[2048,768]{1,0:T(8,128)(2,1)}, bf16[512,1024]{1,0:T(8,128)...) custom-call(bf16[512,768]{1,0:T(8,128)(2,1)} %tok_ref.3, ...), custom_call_target="tpu_custom_call" | custom-call | flops 2013265920 | bytes 41943040 | tf_op jit(solution)/shard_map/forward_attention/pallas_call | solution.py:457
  58.6 43.7 %dense_layers.1 = (bf16[512,768]{1,0:T(8,128)(2,1)}, f32[512,768]{1,0:T(8,128)}, bf16[2048,256]{1,0:T(8,128)(2,1)}, bf16[4,48,3072]{2,1,0:T(8,128)(2,1)}, bf16[4...) custom-call(bf16[512,768]{1,0:T(8,128)(2,1)} %tok_ref.3, ...), custom_call_target="tpu_custom_call" | custom-call | flops 16911433728 | bytes 31457280 | tf_op jit(solution)/shard_map/dense_layers/pallas_call | solution.py:1240
  102.4 1.0 collective-permute-start
  103.4 0.6 collective-permute-start.1
  104.0 24.0 %attend_back.1 = (bf16[2048,256]{1,0:T(8,128)(2,1)}, bf16[12288,384]{1,0:T(8,128)(2,1)}) custom-call(s32[256]{0:T(256)} %get-tuple-element.55.idx_ref, s32[256]{0:T(256)} %get-tuple-element.56.live_ref, bf16[2048,256]{1,0:T(8,128)(2,1)} %get-tuple-element.57.q_ref, bf16[2048,256]{1,0:T(8,128)(2,1)} %get-tuple-element.58.do_ref, bf16[2048,256]{1,0:T(8,128)(2,1)} %bitcast.9, ...), custom_call_target="tpu_custom_call" | custom-call | flops 16106127360 | bytes 18874368 | tf_op jit(solution)/shard_map/attend_back/pallas_call | solution.py:503
  128.0 1.9 collective-permute-done.refs_7_
  129.9 0.0 copy-start
  129.9 0.8 collective-permute-done.1
  130.7 0.2 copy-done
  130.9 79.4 %reduce_all.1 = (f32[512,768]{1,0:T(8,128)}, f32[48,768]{1,0:T(8,128)}, f32[48,768]{1,0:T(8,128)}, f32[48,768]{1,0:T(8,128)}, f32[48,3072]{1,0:T(8,128)}, /*inde...) custom-call(bf16[12288,384]{1,0:T(8,128)(2,1)} %get-tuple-element.62.refs_0_, ...), custom_call_target="tpu_custom_call" | custom-call | flops 4026531840 | bytes 41943040 | tf_op jit(solution)/shard_map/reduce_all/pallas_call | solution.py:910
  210.4 4.8 %finish.1 = (bf16[512,768]{1,0:T(8,128)(2,1)}, f32[512,768]{1,0:T(8,128)}, f32[48,768]{1,0:T(8,128)}, f32[48,768]{1,0:T(8,128)}, f32[48,768]{1,0:T(8,128)}, /*in...) custom-call(bf16[512,768]{1,0:T(8,128)(2,1)} %get-tuple-element.54.r, ...), custom_call_target="tpu_custom_call" | custom-call | tf_op jit(solution)/shard_map/finish/pallas_call | solution.py:1314
Async XLA Ops:
  102.4 27.5 %collective-permute-start = (bf16[4,48,3072]{2,1,0:T(8,128)(2,1)}, bf16[4,48,3072]{2,1,0:T(8,128)(2,1)S(1)}, u32[]{:S(2)}, u32[]{:S(2)}) collective-permute-start(bf16[4,48,3072]{2,1,0:T(8,128)(2,1)} %get-tuple-element.69), channel_id=1, source_target_pairs={{0,4},{1,5},{2,6},{3,7},{4,0},{5,1},{6,2},{7,3},{8,12},{9,13},{10,... | collective-permute-start | bytes 3538952 | tf_op jit(solution)/shard_map/ppermute | solution.py:25
  103.4 27.3 %collective-permute-start.1 = (bf16[8,192,384]{2,1,0:T(8,128)(2,1)}, bf16[8,192,384]{2,1,0:T(8,128)(2,1)}, u32[]{:S(2)}, u32[]{:S(2)}) collective-permute-start(bf16[8,192,384]{2,1,0:T(8,128)(2,1)} %get-tuple-element.73), channel_id=1, source_target_pairs={{0,1},{1,0},{2,3},{3,2},{4,5},{5,4},{6,7},{7,6},{8,9},{9,8},{10,11... | collective-permute-start | bytes 3538952 | tf_op jit(solution)/shard_map/ppermute | solution.py:25
  129.9 1.0 copy-start
